TPU v7x, 32 devices: a whole 2x2x4 slice. The times are simulated.
32 devices in a mesh: band: 2 (over x), img: 4 (over z), fsdp: 4 (over y, core).
Axes of the slice: x: 2, y: 2, z: 4, core: 2. Of those that a mesh axis runs over, the one named last changes fastest.
Arguments:
- block_input: bfloat16 [384, 14, 14, 512], P(('img', 'fsdp'), 'band'), may hold values from -6 to 6
- slot_used: int32 [16, 24], P(('img', 'fsdp')), may hold values from 0 to 1, as said below
- cotangent: bfloat16 [384, 14, 14, 512], P(('img', 'fsdp'), 'band'), may hold values from -6 to 6
- ln1_gain: bfloat16 [512], P('fsdp'), may hold values from 0.25 to 1.75
- ln1_bias: bfloat16 [512], P('fsdp'), may hold values from -3 to 3
- w_qkv: bfloat16 [512, 1536], P('fsdp')
- q_bias: bfloat16 [512], P('fsdp'), may hold values from -3 to 3
- v_bias: bfloat16 [512], P('fsdp'), may hold values from -3 to 3
- rel_table: bfloat16 [16, 169], P('fsdp'), may hold values from -4 to 4
- w_out: bfloat16 [512, 512], P('fsdp'), may hold values from -0.75 to 0.75
- out_bias: bfloat16 [512], P('fsdp'), may hold values from -3 to 3
- ln2_gain: bfloat16 [512], P('fsdp'), may hold values from 0.25 to 1.75
- ln2_bias: bfloat16 [512], P('fsdp'), may hold values from -3 to 3
- w_fc1: bfloat16 [512, 2048], P('fsdp'), may hold values from -0.25 to 0.25
- fc1_bias: bfloat16 [2048], P('fsdp'), may hold values from -3 to 3
- w_fc2: bfloat16 [2048, 512], P('fsdp'), may hold values from -0.125 to 0.125
- fc2_bias: bfloat16 [512], P('fsdp'), may hold values from -3 to 3
Outputs:
- block_output: bfloat16 [384, 14, 14, 512], P(('img', 'fsdp'), 'band')
- input_grad: float32 [384, 14, 14, 512], P(('img', 'fsdp'), 'band')
- ln1_gain_grad: float32 [512], P('fsdp')
- ln1_bias_grad: float32 [512], P('fsdp')
- w_qkv_grad: float32 [512, 1536], P('fsdp')
- q_bias_grad: float32 [512], P('fsdp')
- v_bias_grad: float32 [512], P('fsdp')
- rel_table_grad: float32 [16, 169], P('fsdp')
- w_out_grad: float32 [512, 512], P('fsdp')
- out_bias_grad: float32 [512], P('fsdp')
- ln2_gain_grad: float32 [512], P('fsdp')
- ln2_bias_grad: float32 [512], P('fsdp')
- w_fc1_grad: float32 [512, 2048], P('fsdp')
- fc1_bias_grad: float32 [2048], P('fsdp')
- w_fc2_grad: float32 [2048, 512], P('fsdp')
- fc2_bias_grad: float32 [512], P('fsdp')
Inputs may be any that keep to these rules, and one draw needn't show every extreme that they name: `slot_used`: each row holds between 16 and 24 ones in any positions; both counts occur in every draw.
All inputs are finite; a program needn't handle non-finite values.
Results may differ from a plain program's by a relative error of at most 0.013.
The roundings to bfloat16 on the way count: a program that leaves them out, or rounds other values in their place, can miss the bound.
Values may be sent and summed in bfloat16 or wider, within the bound.
No kernel may reach another device: no remote copies, remote signals or barrier semaphores. Data moves between devices by JAX's collectives and lax.ppermute only.
A program may use at most 320 MiB of HBM per device.

v0:
```python
import jax
import jax.numpy as jnp
from jax import lax
from jax.sharding import PartitionSpec as P

D = 512
HEADS = 16
WIN = 7
SHIFT = 3
SIDE = 14
TABLE = 169


EPSILON = 1e-05
NEGATIVE = -1e30


def from_partner(value, axis, apart):
    mask = 2**apart
    pairs = [(source, source ^ mask) for source in range(lax.axis_size(axis))]
    return lax.ppermute(value, axis, pairs)


def rel_onehot():
    length = WIN * WIN
    places = jnp.arange(length)
    rowpos = places // WIN
    colpos = places % WIN
    index = (rowpos[:, None] - rowpos[None, :] + WIN - 1) * (2 * WIN - 1) + (
        colpos[:, None] - colpos[None, :] + WIN - 1
    )
    return (index.reshape(-1)[:, None] == jnp.arange(TABLE)[None, :]).astype(jnp.float32)


def window_same():
    cells = jnp.arange(SIDE)
    region = jnp.where(cells < SIDE - WIN, 0, jnp.where(cells < SIDE - SHIFT, 1, 2))
    label = region[:, None] * 3 + region[None, :]
    per_image = SIDE // WIN
    label = (
        label.reshape(per_image, WIN, per_image, WIN).transpose(0, 2, 1, 3).reshape(-1, WIN * WIN)
    )
    return label[:, :, None] == label[:, None, :]


def normalize(values):
    center = values - jnp.mean(values, -1, keepdims=True)
    spread = jnp.mean(center * center, -1, keepdims=True)
    rstd = lax.rsqrt(spread + EPSILON)
    return (center * rstd, rstd)


def norm_back(grad_hat, normal, rstd):
    return rstd * (
        grad_hat
        - jnp.mean(grad_hat, -1, keepdims=True)
        - normal * jnp.mean(grad_hat * normal, -1, keepdims=True)
    )


def gelu_slope(pre):
    return (
        0.5 * (1.0 + lax.erf(pre * 0.7071067811865476))
        + pre * jnp.exp(-0.5 * pre * pre) * 0.3989422804014327
    )


def to_windows(tensor):
    count = tensor.shape[0]
    width = tensor.shape[-1]
    return (
        tensor.reshape(count, WIN, SIDE // WIN, WIN, width)
        .transpose(0, 2, 1, 3, 4)
        .reshape(-1, width)
    )


def from_windows(tensor, count):
    width = tensor.shape[-1]
    return (
        tensor.reshape(count, SIDE // WIN, WIN, WIN, width)
        .transpose(0, 2, 1, 3, 4)
        .reshape(count, WIN, SIDE, width)
    )


def attention_logits(queries, keys_win, bias, same):
    scores = jnp.einsum("wqhd,wkhd->whqk", queries, keys_win, preferred_element_type=jnp.float32)
    length = scores.shape[-1]
    scores = scores.reshape(-1, same.shape[0], HEADS, length, length) + bias[None, None]
    scores = jnp.where(same[None, :, None], scores, NEGATIVE)
    return scores.reshape(-1, HEADS, length, length)


def shards(
    block_input,
    slot_used,
    cotangent,
    ln1_gain,
    ln1_bias,
    w_qkv,
    q_bias,
    v_bias,
    rel_table,
    w_out,
    out_bias,
    ln2_gain,
    ln2_bias,
    w_fc1,
    fc1_bias,
    w_fc2,
    fc2_bias,
):
    f32 = jnp.float32
    bf16 = jnp.bfloat16
    (
        gain_low,
        beta_low,
        weight_qkv,
        qbias_low,
        vbias_low,
        table,
        weight_out,
        pbias_low,
        gain2_low,
        beta2_low,
        weight_up,
        ubias_low,
        weight_down,
        dbias_low,
    ) = (
        lax.all_gather(ln1_gain, "fsdp", axis=0, tiled=True),
        lax.all_gather(ln1_bias, "fsdp", axis=0, tiled=True),
        lax.all_gather(w_qkv, "fsdp", axis=0, tiled=True),
        lax.all_gather(q_bias, "fsdp", axis=0, tiled=True),
        lax.all_gather(v_bias, "fsdp", axis=0, tiled=True),
        lax.all_gather(rel_table, "fsdp", axis=0, tiled=True),
        lax.all_gather(w_out, "fsdp", axis=0, tiled=True),
        lax.all_gather(out_bias, "fsdp", axis=0, tiled=True),
        lax.all_gather(ln2_gain, "fsdp", axis=0, tiled=True),
        lax.all_gather(ln2_bias, "fsdp", axis=0, tiled=True),
        lax.all_gather(w_fc1, "fsdp", axis=0, tiled=True),
        lax.all_gather(fc1_bias, "fsdp", axis=0, tiled=True),
        lax.all_gather(w_fc2, "fsdp", axis=0, tiled=True),
        lax.all_gather(fc2_bias, "fsdp", axis=0, tiled=True),
    )
    gain_one = gain_low.astype(f32)
    beta_one = beta_low.astype(f32)
    query_bias = qbias_low.astype(f32)
    value_bias = vbias_low.astype(f32)
    proj_bias = pbias_low.astype(f32)
    gain_two = gain2_low.astype(f32)
    beta_two = beta2_low.astype(f32)
    up_bias = ubias_low.astype(f32)
    down_bias = dbias_low.astype(f32)
    slots = block_input.shape[0]
    length = WIN * WIN
    head_dim = D // HEADS
    scale = head_dim ** (-0.5)
    per_image = SIDE // WIN
    onehot = rel_onehot()
    bias = jnp.dot(table.astype(f32), onehot.T, precision=lax.Precision.HIGHEST).reshape(
        HEADS, length, length
    )
    same = lax.dynamic_slice_in_dim(window_same(), lax.axis_index("band") * per_image, per_image, 0)
    inputs = block_input.astype(f32).reshape(-1, D)
    hat_one, rstd_one = normalize(inputs)
    normed = (hat_one * gain_one + beta_one).astype(bf16).reshape(slots, WIN, SIDE, D)
    arrived = from_partner(normed[:, :SHIFT], "band", 0)
    shifted = jnp.roll(jnp.concatenate([normed[:, SHIFT:], arrived], axis=1), -SHIFT, axis=2)
    windows = to_windows(shifted)
    qkv = jnp.dot(windows, weight_qkv, preferred_element_type=f32)
    queries = ((qkv[:, :D] + query_bias) * scale).astype(bf16).reshape(-1, length, HEADS, head_dim)
    keys_win = qkv[:, D : 2 * D].astype(bf16).reshape(-1, length, HEADS, head_dim)
    values = (qkv[:, 2 * D :] + value_bias).astype(bf16).reshape(-1, length, HEADS, head_dim)
    scores = attention_logits(queries, keys_win, bias, same)
    peak = jnp.max(scores, -1, keepdims=True)
    lse = peak + jnp.log(jnp.sum(jnp.exp(scores - peak), -1, keepdims=True))
    probs = jnp.exp(scores - lse).astype(bf16)
    attended = (
        jnp.einsum("whqk,wkhd->wqhd", probs, values, preferred_element_type=f32)
        .astype(bf16)
        .reshape(-1, D)
    )
    proj = (jnp.dot(attended, weight_out, preferred_element_type=f32) + proj_bias).astype(bf16)
    framed = jnp.roll(from_windows(proj, slots), SHIFT, axis=2)
    returned = from_partner(framed[:, WIN - SHIFT :], "band", 0)
    restored = jnp.concatenate([returned, framed[:, : WIN - SHIFT]], axis=1)
    resid = inputs + restored.astype(f32).reshape(-1, D)
    hat_two, rstd_two = normalize(resid)
    normed_two = (hat_two * gain_two + beta_two).astype(bf16)
    pre = jnp.dot(normed_two, weight_up, preferred_element_type=f32) + up_bias
    act = jax.nn.gelu(pre, approximate=False).astype(bf16)
    mlp_out = jnp.dot(act, weight_down, preferred_element_type=f32) + down_bias
    used_rows = jnp.repeat(slot_used.reshape(-1).astype(f32), WIN * SIDE)[:, None]
    output = (used_rows * (resid + mlp_out)).astype(bf16)
    grad_out = cotangent.astype(f32).reshape(-1, D) * used_rows
    grad_low = grad_out.astype(bf16)
    grad_down = jnp.dot(act.T, grad_low, preferred_element_type=f32)
    grad_downb = jnp.sum(grad_out, 0)
    grad_pre = jnp.dot(grad_low, weight_down.T, preferred_element_type=f32) * gelu_slope(pre)
    grad_upb = jnp.sum(grad_pre, 0)
    grad_hidden = grad_pre.astype(bf16)
    grad_up = jnp.dot(normed_two.T, grad_hidden, preferred_element_type=f32)
    grad_normed_two = jnp.dot(grad_hidden, weight_up.T, preferred_element_type=f32)
    grad_gain_two = jnp.sum(grad_normed_two * hat_two, 0)
    grad_beta_two = jnp.sum(grad_normed_two, 0)
    grad_resid = grad_out + norm_back(grad_normed_two * gain_two, hat_two, rstd_two)
    grad_projb = jnp.sum(grad_resid, 0)
    resid_low = grad_resid.astype(bf16).reshape(slots, WIN, SIDE, D)
    crossed = from_partner(resid_low[:, :SHIFT], "band", 0)
    grad_proj = to_windows(
        jnp.roll(jnp.concatenate([resid_low[:, SHIFT:], crossed], axis=1), -SHIFT, axis=2)
    )
    grad_wout = jnp.dot(attended.T, grad_proj, preferred_element_type=f32)
    grad_attended = (
        jnp.dot(grad_proj, weight_out.T, preferred_element_type=f32)
        .astype(bf16)
        .reshape(-1, length, HEADS, head_dim)
    )
    recomputed = jnp.exp(attention_logits(queries, keys_win, bias, same) - lse)
    grad_probs = jnp.einsum("wqhd,wkhd->whqk", grad_attended, values, preferred_element_type=f32)
    grad_scores = recomputed * (grad_probs - jnp.sum(recomputed * grad_probs, -1, keepdims=True))
    grad_table = jnp.dot(
        jnp.sum(grad_scores, 0).reshape(HEADS, length * length),
        onehot,
        precision=lax.Precision.HIGHEST,
    )
    grad_logits = grad_scores.astype(bf16)
    grad_queries = (
        jnp.einsum("whqk,wkhd->wqhd", grad_logits, keys_win, preferred_element_type=f32).reshape(
            -1, D
        )
        * scale
    )
    grad_keys = jnp.einsum(
        "whqk,wqhd->wkhd", grad_logits, queries, preferred_element_type=f32
    ).reshape(-1, D)
    grad_values = jnp.einsum(
        "whqk,wqhd->wkhd", probs, grad_attended, preferred_element_type=f32
    ).reshape(-1, D)
    grad_qbias = jnp.sum(grad_queries, 0)
    grad_vbias = jnp.sum(grad_values, 0)
    grad_qkv = jnp.concatenate([grad_queries, grad_keys, grad_values], axis=1).astype(bf16)
    grad_wqkv = jnp.dot(windows.T, grad_qkv, preferred_element_type=f32)
    grad_shifted = jnp.dot(grad_qkv, weight_qkv.T, preferred_element_type=f32).astype(bf16)
    grad_framed = jnp.roll(from_windows(grad_shifted, slots), SHIFT, axis=2)
    grad_back = from_partner(grad_framed[:, WIN - SHIFT :], "band", 0)
    grad_normed = (
        jnp.concatenate([grad_back, grad_framed[:, : WIN - SHIFT]], axis=1)
        .astype(f32)
        .reshape(-1, D)
    )
    grad_gain_one = jnp.sum(grad_normed * hat_one, 0)
    grad_beta_one = jnp.sum(grad_normed, 0)
    grad_input = grad_resid + norm_back(grad_normed * gain_one, hat_one, rstd_one)
    final_output = output.reshape(slots, WIN, SIDE, D)
    final_grad = grad_input.reshape(slots, WIN, SIDE, D)
    s01, s02, s03, s04, s05, s06, s07, s08, s09, s10, s11, s12, s13, s14 = lax.psum(
        (
            grad_gain_one,
            grad_beta_one,
            grad_wqkv,
            grad_qbias,
            grad_vbias,
            grad_table,
            grad_wout,
            grad_projb,
            grad_gain_two,
            grad_beta_two,
            grad_up,
            grad_upb,
            grad_down,
            grad_downb,
        ),
        ("band", "img"),
    )
    r01, r02, r03, r04, r05, r06, r07, r08, r09, r10, r11, r12, r13, r14 = (
        lax.psum_scatter(s01, "fsdp", scatter_dimension=0, tiled=True),
        lax.psum_scatter(s02, "fsdp", scatter_dimension=0, tiled=True),
        lax.psum_scatter(s03, "fsdp", scatter_dimension=0, tiled=True),
        lax.psum_scatter(s04, "fsdp", scatter_dimension=0, tiled=True),
        lax.psum_scatter(s05, "fsdp", scatter_dimension=0, tiled=True),
        lax.psum_scatter(s06, "fsdp", scatter_dimension=0, tiled=True),
        lax.psum_scatter(s07, "fsdp", scatter_dimension=0, tiled=True),
        lax.psum_scatter(s08, "fsdp", scatter_dimension=0, tiled=True),
        lax.psum_scatter(s09, "fsdp", scatter_dimension=0, tiled=True),
        lax.psum_scatter(s10, "fsdp", scatter_dimension=0, tiled=True),
        lax.psum_scatter(s11, "fsdp", scatter_dimension=0, tiled=True),
        lax.psum_scatter(s12, "fsdp", scatter_dimension=0, tiled=True),
        lax.psum_scatter(s13, "fsdp", scatter_dimension=0, tiled=True),
        lax.psum_scatter(s14, "fsdp", scatter_dimension=0, tiled=True),
    )
    return (
        final_output,
        final_grad,
        r01,
        r02,
        r03,
        r04,
        r05,
        r06,
        r07,
        r08,
        r09,
        r10,
        r11,
        r12,
        r13,
        r14,
    )


def solution(mesh):
    placed = (
        P(("img", "fsdp"), "band", None, None),
        P(("img", "fsdp"), None),
        P(("img", "fsdp"), "band", None, None),
        P("fsdp"),
        P("fsdp"),
        P("fsdp", None),
        P("fsdp"),
        P("fsdp"),
        P("fsdp", None),
        P("fsdp", None),
        P("fsdp"),
        P("fsdp"),
        P("fsdp"),
        P("fsdp", None),
        P("fsdp"),
        P("fsdp", None),
        P("fsdp"),
    )
    return jax.shard_map(
        shards,
        mesh=mesh,
        in_specs=placed,
        out_specs=(
            P(("img", "fsdp"), "band", None, None),
            P(("img", "fsdp"), "band", None, None),
            P("fsdp"),
            P("fsdp"),
            P("fsdp", None),
            P("fsdp"),
            P("fsdp"),
            P("fsdp", None),
            P("fsdp", None),
            P("fsdp"),
            P("fsdp"),
            P("fsdp"),
            P("fsdp", None),
            P("fsdp"),
            P("fsdp", None),
            P("fsdp"),
        ),
        check_vma=False,
    )
```

profile of v0, /device:TPU:0, one launch (start us, length us, event | category | flops | bytes accessed | tf_op | source)
XLA Modules:
  0.0 890.9 jit_solution(15372807008228085413)
XLA Ops:
  84.7 11.5 %reshape.462 = bf16[48,49,16,32]{3,2,1,0:T(8,128)(2,1)} reshape(bf16[2352,512]{1,0:T(8,128)(2,1)} %get-tuple-element.117) | data formatting | bytes 4816896 | tf_op jit(solution)/shard_map/reshape | solution.py:173
  96.2 13.5 %copy.127 = bf16[48,49,16,32]{1,3,2,0:T(8,128)(2,1)} copy(bf16[48,49,16,32]{3,2,1,0:T(8,128)(2,1)} %reshape.462) | data formatting | bytes 4816896 | tf_op jit(solution)/shard_map/reshape | solution.py:173
  109.8 11.5 %reshape.463 = bf16[48,49,16,32]{3,2,1,0:T(8,128)(2,1)} reshape(bf16[2352,512]{1,0:T(8,128)(2,1)} %slice.113) | data formatting | bytes 4816896 | tf_op jit(solution)/shard_map/reshape | solution.py:174
  121.3 13.5 %copy.128 = bf16[48,49,16,32]{1,3,2,0:T(8,128)(2,1)} copy(bf16[48,49,16,32]{3,2,1,0:T(8,128)(2,1)} %reshape.463) | data formatting | bytes 4816896 | tf_op jit(solution)/shard_map/reshape | solution.py:174
  134.9 13.4 %fusion.15 = (f32[48,16,49]{2,1,0:T(8,128)S(1)}, f32[48,16,49,49]{2,3,1,0:T(8,128)}) fusion(f32[16,49,49]{1,2,0:T(8,128)S(1)} %copy.129, pred[48,49,49]{1,2,0:T(8,128)(4,1)S(1)} %bitcast.95, bf16[48,49,16,32]{1,3,2,0:T(8,128)(2,1)} %copy.127, bf16[48,49,16,32]{1,3,2,0:T(8,128)(2,1)} %copy.128), kind=kOutput, calls=%fused_computation.30 | convolution fusion | flops 123508224 | bytes 12612208 | tf_op jit(solution)/shard_map/wqhd,wkhd->whqk/dot_general | solution.py:88
  148.3 13.4 %exponential_reduce_fusion = f32[48,16,49]{2,1,0:T(8,128)S(1)} fusion(f32[48,16,49,49]{2,3,1,0:T(8,128)} %get-tuple-element.122, f32[48,16,49]{2,1,0:T(8,128)S(1)} %get-tuple-element.121, f32[16,49,49]{1,2,0:T(8,128)S(1)} %copy.129, pred[48,49,49]{1,2,0:T(8,128)(4,1)S(1)} %bitcast.96), kind=kLoop, calls=%fused_computation.5 | loop fusion | flops 7338240 | bytes 7945840 | tf_op jit(solution)/shard_map/reduce_sum | solution.py:178
  162.5 11.5 %reshape.461 = bf16[48,49,16,32]{3,2,1,0:T(8,128)(2,1)} reshape(bf16[2352,512]{1,0:T(8,128)(2,1)} %get-tuple-element.118) | data formatting | bytes 4816896 | tf_op jit(solution)/shard_map/reshape | solution.py:175
  174.0 13.5 %copy.130 = bf16[48,49,16,32]{1,3,2,0:T(8,128)(2,1)} copy(bf16[48,49,16,32]{3,2,1,0:T(8,128)(2,1)} %reshape.461) | data formatting | bytes 4816896 | tf_op jit(solution)/shard_map/reshape | solution.py:175
  187.6 14.4 %convert_bitcast_fusion.1 = bf16[48,49,16,32]{1,3,2,0:T(8,128)(2,1)} fusion(bf16[48,49,16,32]{1,3,2,0:T(8,128)(2,1)} %copy.130, f32[48,16,49,49]{2,3,1,0:T(8,128)} %get-tuple-element.122, f32[48,16,49]{2,1,0:T(8,128)} %log_add_fusion, f32[16,49,49]{1,2,0:T(8,128)S(1)} %copy.129, pred[48,49,49]{1,2,0:T(8,128)(4,1)S(1)} %bitcast.97), kind=kOutput, calls=%fused_computation.38 | convolution fusion | flops 126594048 | bytes 12612208 | tf_op jit(solution)/shard_map/whqk,wkhd->wqhd/dot_general | solution.py:181
  201.9 9.5 %copy.132 = bf16[48,49,16,32]{1,0,3,2:T(8,128)(2,1)} copy(bf16[48,49,16,32]{1,3,2,0:T(8,128)(2,1)} %convert_bitcast_fusion.1) | data formatting | bytes 4816896 | tf_op jit(solution)/shard_map/convert_element_type | solution.py:182
  300.0 49.9 %fusion.2 = (bf16[2352,2048]{1,0:T(8,128)(2,1)}, f32[2352,2048]{1,0:T(8,128)}) fusion(f32[2048]{0:T(1024)S(1)} %bitcast.122, bf16[512,2048]{1,0:T(8,128)(2,1)} %all-gather.16.cloned.1.call-done, f32[2352,512]{1,0:T(8,128)} %add.283, f32[512]{0:T(512)S(1)} %bitcast.125, f32[512]{0:T(512)S(1)} %bitcast.115, f32[2352]{0:T(1024)S(1)} %rsqrt.25, f32[2352]{0:T(1024)S(1)} %div.52), kind=kOutput, calls=%fused_computation.9 | convolution fusion | flops 5256437760 | bytes 35846528 | tf_op jit(solution)/shard_map/dot_general | solution.py:192
  349.9 18.1 %fusion.50 = (f32[2048]{0:T(1024)}, bf16[2352,2048]{1,0:T(8,128)(2,1)}) fusion(f32[2352,2048]{1,0:T(8,128)} %get-tuple-element.124, f32[2048]{0:T(1024)S(1)} %bitcast.123, bf16[2048,512]{1,0:T(8,128)(2,1)} %all-gather.18.cloned.1.call-done, f32[2352,512]{1,0:T(8,128)} %reshape.409, f32[2352]{0:T(1024)S(1)} %copy-done.31), kind=kOutput, calls=%fused_computation.130 | convolution fusion | flops 4992710656 | bytes 35841216 | tf_op jit(solution)/shard_map/dot_general | solution.py:201
  368.0 12.3 %multiply_reduce_fusion.3 = (f32[512]{0:T(512)}, f32[2352]{0:T(1024)S(1)}, f32[2352]{0:T(1024)S(1)}, f32[512]{0:T(512)}, f32[2352,512]{1,0:T(8,128)S(1)}) fusion(f32[2352,512]{1,0:T(8,128)S(1)} %copy-done.9, f32[2352]{0:T(1024)S(1)} %rsqrt.25, f32[2352]{0:T(1024)S(1)} %div.52, f32[512]{0:T(512)S(1)} %bitcast.116, bf16[512,2048]{1,0:T(8,128)(2,1)S(1)} %copy-done.56, ...), kind=kOutput, calls=%fused_computation.51 | convolution fusion | flops 4943333376 | bytes 21408512 | tf_op jit(solution)/shard_map/dot_general | solution.py:205
  393.5 23.3 %collective-permute-done.2 = bf16[24,3,14,512]{3,0,2,1:T(8,128)(2,1)S(1)} collective-permute-done((bf16[24,3,14,512]{3,0,2,1:T(8,128)(2,1)S(1)}, bf16[24,3,14,512]{3,0,2,1:T(8,128)(2,1)S(1)}, u32[]{:S(2)}, u32[]{:S(2)}) %collective-permute-start.2) | collective-permute-done | bytes 1032224 | tf_op jit(solution)/shard_map/ppermute | solution.py:21
  431.4 11.5 %reshape.464 = bf16[48,49,16,32]{3,2,1,0:T(8,128)(2,1)} reshape(bf16[2352,512]{1,0:T(8,128)(2,1)} %convolution_convert_fusion.1) | data formatting | bytes 4816896 | tf_op jit(solution)/shard_map/reshape | solution.py:219
  442.9 13.6 %copy.144 = bf16[48,49,16,32]{1,3,2,0:T(8,128)(2,1)} copy(bf16[48,49,16,32]{3,2,1,0:T(8,128)(2,1)} %reshape.464) | data formatting | bytes 4816896 | tf_op jit(solution)/shard_map/reshape | solution.py:219
  456.6 23.3 %multiply_reduce_fusion = (f32[48,16,49]{2,1,0:T(8,128)S(1)}, f32[48,16,49,49]{2,3,1,0:T(8,128)}) fusion(f32[48,16,49,49]{2,3,1,0:T(8,128)} %get-tuple-element.122, f32[48,16,49]{2,1,0:T(8,128)S(1)} %copy-done.8, f32[16,49,49]{1,2,0:T(8,128)S(1)} %copy-done.3, pred[48,49,49]{1,2,0:T(8,128)(4,1)S(1)} %bitcast.98, bf16[48,49,16,32]{1,3,2,0:T(8,128)(2,1)} %copy.144, ...), kind=kOutput, calls=%fused_computation.3 | convolution fusion | flops 127196160 | bytes 20138608 | tf_op jit(solution)/shard_map/wqhd,wkhd->whqk/dot_general | solution.py:222
  479.9 19.4 %bitcast_convert_fusion = (bf16[48,49,16,32]{1,3,2,0:T(8,128)(2,1)}, f32[48,16,32,49]{3,2,1,0:T(8,128)}) fusion(bf16[48,49,16,32]{1,3,2,0:T(8,128)(2,1)} %copy.144, f32[48,16,49,49]{2,3,1,0:T(8,128)} %get-tuple-element.122, f32[48,16,49]{2,1,0:T(8,128)S(1)} %copy-done.8, f32[16,49,49]{1,2,0:T(8,128)S(1)} %copy-done.3, pred[48,49,49]{1,2,0:T(8,128)(4,1)S(1)} %bitcast.99), kind=kOutput, calls=%fused_computation.32 | convolution fusion | flops 126594048 | bytes 17429104 | tf_op jit(solution)/shard_map/whqk,wqhd->wkhd/dot_general | solution.py:239
  499.2 21.2 %fusion.48 = (f32[16,49,49]{1,2,0:T(8,128)}, bf16[48,16,49,49]{2,3,1,0:T(8,128)(2,1)}) fusion(f32[48,16,49,49]{2,3,1,0:T(8,128)} %get-tuple-element.127, f32[48,16,49]{2,1,0:T(8,128)S(1)} %get-tuple-element.126, f32[48,16,49]{2,1,0:T(8,128)S(1)} %copy-done.8, f32[48,16,49,49]{2,3,1,0:T(8,128)} %get-tuple-element.122, f32[16,49,49]{1,2,0:T(8,128)S(1)} %copy-done.3, ...), kind=kLoop, calls=%fused_computation.129 | loop fusion | flops 12869360 | bytes 19163312 | tf_op jit(solution)/shard_map/reduce_sum | solution.py:225
  520.4 10.4 %convert_bitcast_fusion = bf16[48,49,16,32]{1,3,2,0:T(8,128)(2,1)} fusion(bf16[48,49,16,32]{1,3,2,0:T(8,128)(2,1)S(1)} %bitcast.94, bf16[48,16,49,49]{2,3,1,0:T(8,128)(2,1)} %get-tuple-element.115), kind=kOutput, calls=%fused_computation.37 | convolution fusion | flops 119218176 | bytes 8504832 | tf_op jit(solution)/shard_map/whqk,wqhd->wkhd/dot_general | solution.py:236
  530.8 11.9 %multiply_reduce_fusion.1 = (f32[16,32]{1,0:T(8,128)S(1)}, bf16[48,49,16,32]{1,3,2,0:T(8,128)(2,1)}) fusion(bf16[48,49,16,32]{1,3,2,0:T(8,128)(2,1)} %copy.128, bf16[48,16,49,49]{2,3,1,0:T(8,128)(2,1)} %get-tuple-element.115), kind=kOutput, calls=%fused_computation.33 | convolution fusion | flops 121626112 | bytes 8506880 | tf_op jit(solution)/shard_map/whqk,wkhd->wqhd/dot_general | solution.py:231
  542.8 9.6 %copy.151 = bf16[48,49,16,32]{1,0,3,2:T(8,128)(2,1)} copy(bf16[48,49,16,32]{1,3,2,0:T(8,128)(2,1)} %convert_bitcast_fusion) | data formatting | bytes 4816896 | tf_op jit(solution)/shard_map/whqk,wqhd->wkhd/transpose | solution.py:236
  560.8 9.6 %copy.154 = bf16[48,49,16,32]{1,0,3,2:T(8,128)(2,1)} copy(bf16[48,49,16,32]{1,3,2,0:T(8,128)(2,1)} %get-tuple-element.128) | data formatting | bytes 4816896 | tf_op jit(solution)/shard_map/convert.5
  579.6 9.4 %copy.148 = bf16[48,49,16,32]{1,0,3,2:T(8,128)(2,1)} copy(bf16[48,49,16,32]{1,3,2,0:T(8,128)(2,1)} %get-tuple-element.120) | data formatting | bytes 4816896 | tf_op jit(solution)/shard_map/mul | solution.py:231
  610.2 11.0 %fusion.42 = f32[2048,512]{1,0:T(8,128)} fusion(bf16[2352,2048]{1,0:T(8,128)(2,1)} %get-tuple-element.123, f32[2352,512]{1,0:T(8,128)} %reshape.409, f32[2352]{0:T(1024)S(1)} %copy-done.32), kind=kOutput, calls=%fused_computation.125 | convolution fusion | flops 4934909952 | bytes 18654400 | tf_op jit(solution)/shard_map/dot_general | solution.py:199
  621.6 13.1 %fusion.25 = f32[512,2048]{1,0:T(8,128)} fusion(bf16[2352,2048]{1,0:T(8,128)(2,1)} %get-tuple-element.131, f32[2352,512]{1,0:T(8,128)} %add.283, f32[512]{0:T(512)S(1)} %bitcast.126, f32[512]{0:T(512)S(1)} %bitcast.118, f32[2352]{0:T(1024)S(1)} %copy-done.28, f32[2352]{0:T(1024)S(1)} %copy-done.30), kind=kOutput, calls=%fused_computation.57 | convolution fusion | flops 4938522624 | bytes 18667904 | tf_op jit(solution)/shard_map/dot_general | solution.py:204
  662.7 10.6 %multiply_convert_fusion.1 = bf16[2352,512]{1,0:T(8,128)(2,1)} fusion(f32[2352,512]{1,0:T(8,128)S(1)} %bitcast.102, bf16[2352,2048]{1,0:T(8,128)(2,1)} %get-tuple-element.123, bf16[2048,512]{1,0:T(8,128)(2,1)S(1)} %copy-done.55, f32[512]{0:T(512)S(1)} %bitcast.128, f32[2352]{0:T(1024)S(1)} %copy-done.32), kind=kOutput, calls=%fused_computation.61 | convolution fusion | flops 4937318400 | bytes 18967744 | tf_op jit(solution)/shard_map/dot_general | solution.py:194
  681.2 15.3 %reduce-scatter.11.cloned.1.call-done = f32[512,512]{1,0:T(8,128)} async-done(((f32[2048,512]{1,0:T(8,128)}), f32[512,512]{1,0:T(8,128)}) %reduce-scatter.11.cloned.1.call-update) | async-done | bytes 1048592 | tf_op jit(solution)/shard_map/reduce_scatter | solution.py:291
  696.5 47.1 %reduce-scatter.9.cloned.1.call-done = f32[128,2048]{1,0:T(8,128)} async-done(((f32[512,2048]{1,0:T(8,128)}), f32[128,2048]{1,0:T(8,128)}) %reduce-scatter.9.cloned.1.call-update) | async-done | bytes 1048592 | tf_op jit(solution)/shard_map/reduce_scatter | solution.py:289
  755.9 11.6 %all-reduce.12 = (f32[512]{0:T(512)S(1)}, f32[512]{0:T(512)S(1)}, f32[512]{0:T(512)S(1)}, f32[512]{0:T(512)S(1)}, f32[16,169]{1,0:T(8,128)S(1)}, /*index=5*/f32[...) all-reduce(f32[512]{0:T(512)S(1)} %get-tuple-element.82, ...), channel_id=2, replica_groups=mesh['band'=2,'img'=4,'fsdp'=4] {'fsdp'}, use_global_device_ids=true, to_apply=%region_13.14.clone | all-reduce | flops 8848 | bytes 70784
  802.3 37.5 %all-reduce.10 = (f32[128]{0:T(128)}, f32[128]{0:T(128)}, f32[128]{0:T(128)}, f32[128]{0:T(128)}, f32[4,169]{1,0:T(4,128)}, /*index=5*/f32[128]{0:T(128)}, f32[1...) all-reduce(f32[128]{0:T(128)S(1)} %dynamic-slice.1, ...), channel_id=1, replica_groups=mesh['band'=2,'img'=4,'fsdp'=4] {'band','img'}, use_global_device_ids=true, to_apply=%region_12.13 | all-reduce | flops 2212 | bytes 17696 | tf_op jit(solution)/shard_map/psum | solution.py:259
  839.8 36.6 %all-reduce.15.cloned.1.call-done = (f32[128,1536]{1,0:T(8,128)}, f32[128,512]{1,0:T(8,128)}, f32[128,2048]{1,0:T(8,128)}, f32[512,512]{1,0:T(8,128)}) async-done(((f32[128,1536]{1,0:T(8,128)}, f32[128,512]{1,0:T(8,128)}, f32[128,2048]{1,0:T(8,128)}, f32[512,512]{1,0:T(8,128)}), (f32[128,1536]{1,0:T(8,128)}, f32[128,512]{1,0:T(8,128)}, f32[128,2048]{1,0:T(8,128)}, ...) | async-done | bytes 3145744 | tf_op jit(solution)/shard_map/psum | solution.py:259
  (300 shorter events, 321.3 us)
Async XLA Ops:
  7.2 17.4 %copy-start = (bf16[24,7,14,512]{3,0,2,1:T(8,128)(2,1)S(1)}, bf16[24,7,14,512]{3,0,2,1:T(8,128)(2,1)}, u32[]{:S(2)}) copy-start(bf16[24,7,14,512]{3,0,2,1:T(8,128)(2,1)} %param.17) | copy-start | bytes 7225348
  7.2 65.9 %all-gather.14.cloned.1.call-start = ((), (), s32[]{:S(2)}) async-start(), calls=%async_computation.4 | async-start | bytes 1966080 | tf_op jit(solution)/shard_map/all_gather | solution.py:134
  7.9 292.1 %all-gather.16.cloned.1.call-start = ((), (), s32[]{:S(2)}) async-start(), calls=%async_computation.5 | async-start | bytes 2621440 | tf_op jit(solution)/shard_map/all_gather | solution.py:142
  24.7 18.1 %copy-start.51 = (bf16[128]{0:T(256)(128)(2,1)S(1)}, bf16[128]{0:T(256)(128)(2,1)}, u32[]{:S(2)}) copy-start(bf16[128]{0:T(256)(128)(2,1)} %param.27) | copy-start | bytes 772
  24.7 23.3 %copy-start.43 = (bf16[4,169]{1,0:T(4,128)(2,1)S(1)}, bf16[4,169]{1,0:T(4,128)(2,1)}, u32[]{:S(2)}) copy-start(bf16[4,169]{1,0:T(4,128)(2,1)} %param.25) | copy-start | bytes 4060
  27.2 27.6 %copy-start.26 = (bf16[128,512]{1,0:T(8,128)(2,1)S(1)}, bf16[128,512]{1,0:T(8,128)(2,1)}, u32[]{:S(2)}) copy-start(bf16[128,512]{1,0:T(8,128)(2,1)} %param.26) | copy-start | bytes 393220
  28.2 34.5 %collective-permute-start = (bf16[24,3,14,512]{3,0,2,1:T(8,128)(2,1)}, bf16[24,3,14,512]{3,0,2,1:T(8,128)(2,1)}, u32[]{:S(2)}, u32[]{:S(2)}) collective-permute-start(bf16[24,3,14,512]{3,0,2,1:T(8,128)(2,1)} %slice.82), channel_id=1, source_target_pairs={{0,16},{16,0},{1,17},{17,1},{2,18},{18,2},{3,19},{19,3},{4,20},{20... | collective-permute-start | bytes 3096584 | tf_op jit(solution)/shard_map/ppermute | solution.py:21
  30.0 319.9 %all-gather.18.cloned.1.call-start = ((), (), s32[]{:S(2)}) async-start(), calls=%async_computation.6 | async-start | bytes 2621440 | tf_op jit(solution)/shard_map/all_gather | solution.py:144
  54.7 132.9 %copy-start.2 = (f32[16,49,49]{1,2,0:T(8,128)}, f32[16,49,49]{1,2,0:T(8,128)S(1)}, u32[]{:S(2)}) copy-start(f32[16,49,49]{1,2,0:T(8,128)S(1)} %copy.129) | copy-start | bytes 460996
  134.9 52.7 %copy-start.6 = (pred[24,2,49,49]{2,3,1,0:T(8,128)(4,1)}, pred[24,2,49,49]{2,3,1,0:T(8,128)(4,1)S(1)}, u32[]{:S(2)}) copy-start(pred[24,2,49,49]{2,3,1,0:T(8,128)(4,1)S(1)} %broadcast_in_dim.38) | copy-start | bytes 345748
  236.1 14.0 %copy-start.48 = (bf16[512]{0:T(512)(128)(2,1)S(1)}, bf16[512]{0:T(512)(128)(2,1)}, u32[]{:S(2)}) copy-start(bf16[512]{0:T(512)(128)(2,1)} %param.31) | copy-start | bytes 3076
  236.1 19.5 %copy-start.57 = (s32[1,24]{1,0:T(1,128)S(1)}, s32[1,24]{1,0:T(1,128)}, u32[]{:S(2)}) copy-start(s32[1,24]{1,0:T(1,128)} %param.18) | copy-start | bytes 292
  236.1 37.8 %collective-permute-start.1 = (bf16[24,3,14,512]{3,0,2,1:T(8,128)(2,1)}, bf16[24,3,14,512]{3,0,2,1:T(8,128)(2,1)}, u32[]{:S(2)}, u32[]{:S(2)}) collective-permute-start(bf16[24,3,14,512]{3,0,2,1:T(8,128)(2,1)} %pad_maximum_fusion.5), channel_id=1, source_target_pairs={{0,16},{16,0},{1,17},{17,1},{2,18},{18,2},{3,19},{19,3},{4,20},{20... | collective-permute-start | bytes 3096584 | tf_op jit(solution)/shard_map/ppermute | solution.py:21
  236.6 444.6 %reduce-scatter.7.cloned.1.call-start = ((), (), s32[]{:S(2)}) async-start(), calls=%async_computation.8 | async-start | bytes 1310720 | tf_op jit(solution)/shard_map/reduce_scatter | solution.py:285
  245.1 135.2 %copy-start.38 = (f32[4,1,128]{2,1,0:T(1,128)}, f32[4,1,128]{2,1,0:T(1,128)S(1)}, u32[]{:S(2)}) copy-start(f32[4,1,128]{2,1,0:T(1,128)S(1)} %convert_element_type.158) | copy-start | bytes 6148
  250.1 49.9 %copy-start.46 = (f32[4,1,128]{2,1,0:T(1,128)}, f32[4,1,128]{2,1,0:T(1,128)S(1)}, u32[]{:S(2)}) copy-start(f32[4,1,128]{2,1,0:T(1,128)S(1)} %convert_element_type.159) | copy-start | bytes 6148
  279.2 101.2 %copy-start.27 = (f32[2352]{0:T(1024)}, f32[2352]{0:T(1024)S(1)}, u32[]{:S(2)}) copy-start(f32[2352]{0:T(1024)S(1)} %rsqrt.25) | copy-start | bytes 28228
  279.3 101.0 %copy-start.29 = (f32[2352]{0:T(1024)}, f32[2352]{0:T(1024)S(1)}, u32[]{:S(2)}) copy-start(f32[2352]{0:T(1024)S(1)} %div.52) | copy-start | bytes 28228
  300.0 49.9 %copy-start.31 = (f32[2352]{0:T(1024)S(1)}, f32[2352]{0:T(1024)}, u32[]{:S(2)}) copy-start(f32[2352]{0:T(1024)} %mul.209) | copy-start | bytes 28228
  349.9 18.1 %copy-start.9 = (f32[2352,512]{1,0:T(8,128)S(1)}, f32[2352,512]{1,0:T(8,128)}, u32[]{:S(2)}) copy-start(f32[2352,512]{1,0:T(8,128)} %add.283) | copy-start | bytes 14450692
  349.9 18.1 %copy-start.56 = (bf16[512,2048]{1,0:T(8,128)(2,1)S(1)}, bf16[512,2048]{1,0:T(8,128)(2,1)}, u32[]{:S(2)}) copy-start(bf16[512,2048]{1,0:T(8,128)(2,1)} %all-gather.16.cloned.1.call-done) | copy-start | bytes 6291460
  391.6 25.1 %collective-permute-start.2 = (bf16[24,3,14,512]{3,0,2,1:T(8,128)(2,1)S(1)}, bf16[24,3,14,512]{3,0,2,1:T(8,128)(2,1)S(1)}, u32[]{:S(2)}, u32[]{:S(2)}) collective-permute-start(bf16[24,3,14,512]{3,0,2,1:T(8,128)(2,1)S(1)} %copy.139), channel_id=1, source_target_pairs={{0,16},{16,0},{1,17},{17,1},{2,18},{18,2},{3,19},{19,3},{4,20},{20... | collective-permute-start | bytes 3096584 | tf_op jit(solution)/shard_map/ppermute | solution.py:21
  456.6 63.9 %slice-start = ((s8[6291456]{0:T(1024)(128)(4,1)}), s8[2097152]{0:T(1024)(128)(4,1)S(1)}, s32[]{:S(2)}) async-start(s8[6291456]{0:T(1024)(128)(4,1)} %bitcast.93), calls=%async_computation.12 | async-start | bytes 4194304
  479.9 40.6 %slice-start.1 = ((s8[6291456]{0:T(1024)(128)(4,1)}), s8[4194304]{0:T(1024)(128)(4,1)S(1)}, s32[]{:S(2)}) async-start(s8[6291456]{0:T(1024)(128)(4,1)} %bitcast.93), calls=%async_computation.13 | async-start | bytes 8388608
  542.7 138.5 %reduce-scatter.5.cloned.1.call-start = ((), (), s32[]{:S(2)}) async-start(), calls=%async_computation.7 | async-start | bytes 3932160 | tf_op jit(solution)/shard_map/reduce_scatter | solution.py:281
  610.1 86.4 %reduce-scatter.11.cloned.1.call-start = ((), (), s32[]{:S(2)}) async-start(), calls=%async_computation.10 | async-start | bytes 5242880 | tf_op jit(solution)/shard_map/reduce_scatter | solution.py:291
  621.3 13.8 %copy-start.58 = (u32[32]{0:T(128)S(1)}, u32[32]{0:T(128)}, u32[]{:S(2)}) copy-start(u32[32]{0:T(128)} %constant.138) | copy-start | bytes 388
  621.3 16.4 %copy-start.54 = (bf16[128]{0:T(256)(128)(2,1)S(1)}, bf16[128]{0:T(256)(128)(2,1)}, u32[]{:S(2)}) copy-start(bf16[128]{0:T(256)(128)(2,1)} %param.33) | copy-start | bytes 772
  621.3 21.8 %copy-start.42 = (f32[24]{0:T(128)S(1)}, f32[24]{0:T(128)}, u32[]{:S(2)}) copy-start(f32[24]{0:T(128)} %copy-done.41) | copy-start | bytes 292
  621.3 122.3 %reduce-scatter.9.cloned.1.call-start = ((), (), s32[]{:S(2)}) async-start(), calls=%async_computation.9 | async-start | bytes 5242880 | tf_op jit(solution)/shard_map/reduce_scatter | solution.py:289
  634.8 241.7 %all-reduce.15.cloned.1.call-start = ((), (), s32[]{:S(2)}) async-start(), calls=%async_computation.11 | async-start | bytes 6291456 | tf_op jit(solution)/shard_map/psum | solution.py:259
  661.1 89.4 %collective-permute-start.3 = (bf16[24,3,14,512]{3,0,2,1:T(8,128)(2,1)}, bf16[24,3,14,512]{3,0,2,1:T(8,128)(2,1)}, u32[]{:S(2)}, u32[]{:S(2)}) collective-permute-start(bf16[24,3,14,512]{3,0,2,1:T(8,128)(2,1)} %pad_maximum_fusion.4), channel_id=1, source_target_pairs={{0,16},{16,0},{1,17},{17,1},{2,18},{18,2},{3,19},{19,3},{4,20},{20... | collective-permute-start | bytes 3096584 | tf_op jit(solution)/shard_map/ppermute | solution.py:21
  (43 other events, 324.0 us)
Sparse Core Ops, SparseCore 0:
  9.6 22.3 all-gather.13
  33.5 22.6 all-gather.15
  236.7 23.8 all-gather.17
  542.8 26.1 reduce-scatter.6
  610.2 39.2 reduce-scatter.4
  651.9 44.5 reduce-scatter.10
  699.0 44.5 reduce-scatter.8
  747.5 128.8 all-reduce.14
where the time goes:
time: 901 us; the launch traced here: 891 us
  local copies, waits for them, and re-layouts  300 us (33%)
  matrix products  243 us (27%)
  waiting for transfers between devices  123 us (14%)
  blocking collectives  110 us (12%)
  other arithmetic  90.6 us (10%)
  between operations  17.6 us (2%)
    dot_general x1, matrix products, shards(): pre = jnp.dot(normed_two, weight_up, preferred_element_type=f32) + up_bias  49.9 us
    reduce_scatter x1, waiting for transfers between devices, shards(): lax.psum_scatter(s11, 'fsdp', scatter_dimension=0, tiled=True)  47.1 us
    psum x1, blocking collectives, shards(): lax.psum((grad_gain_one, grad_beta_one, grad_wqkv, grad_qbias, grad_vbias...  37.5 us
    psum x1, waiting for transfers between devices, shards(): lax.psum((grad_gain_one, grad_beta_one, grad_wqkv, grad_qbias, grad_vbias...  36.6 us
    unnamed x147, local copies, waits for them, and re-layouts  30.9 us
    reshape x2, local copies, waits for them, and re-layouts, shards(): grad_attended = jnp.dot(grad_proj, weight_out.T, preferred_element_type=f...  25.1 us
    reshape x2, local copies, waits for them, and re-layouts, shards(): ((qkv[:, :D] + query_bias) * scale).astype(bf16)  25 us
    reshape x2, local copies, waits for them, and re-layouts, shards(): (qkv[:, 2 * D:] + value_bias).astype(bf16)  25 us
  transfers between devices with their start and end apart: 12, of which 4 were waited for; matrix products, arithmetic and copies ran while one was open for 51% of the time, Pallas kernels for 0%

commit v1 on v0

v1 whole, which is shorter than its diff:
```python
import functools

import jax
import jax.numpy as jnp
from jax import lax
from jax.experimental import pallas as pl
from jax.experimental.pallas import tpu as pltpu
from jax.sharding import PartitionSpec as P

D = 512
HEADS = 16
WIN = 7
SHIFT = 3
SIDE = 14
TABLE = 169
LEN = WIN * WIN
EPSILON = 1e-05
NEGATIVE = -1e30

PAD = 56
SEG = 64
PIC = 2 * PAD
COLS = 16
QUAD = 4
GROUPS = HEADS // QUAD
LANES = 128
HEAD = D // HEADS
SCALE = HEAD ** (-0.5)
OWN = WIN - SHIFT

f32 = jnp.float32
bf16 = jnp.bfloat16


def partner(value, axis, bit):
    mask = 1 << bit
    pairs = [(source, source ^ mask) for source in range(lax.axis_size(axis))]
    return lax.ppermute(value, axis, pairs)


def bits_of(axis):
    return (lax.axis_size(axis) - 1).bit_length()


def nt(left, right):
    return lax.dot_general(left, right, (((1,), (1,)), ((), ())), preferred_element_type=f32)


def nn(left, right):
    return jnp.dot(left, right, preferred_element_type=f32)


def tn(left, right):
    return lax.dot_general(left, right, (((0,), (0,)), ((), ())), preferred_element_type=f32)


def stats(values):
    center = values - jnp.mean(values, -1, keepdims=True)
    rstd = lax.rsqrt(jnp.mean(center * center, -1, keepdims=True) + EPSILON)
    return center * rstd, rstd


def norm_back(grad_hat, normal, rstd):
    return rstd * (
        grad_hat
        - jnp.mean(grad_hat, -1, keepdims=True)
        - normal * jnp.mean(grad_hat * normal, -1, keepdims=True)
    )


def rowsum(values):
    return jnp.sum(values, 0, keepdims=True)


def load_shards(owners, refs, target, sems):
    rows = refs[0].shape[0]
    copies = []
    for at, ref in enumerate(refs):
        start = pl.multiple_of(owners[at] * rows, rows)
        copies.append(pltpu.make_async_copy(ref, target.at[pl.ds(start, rows)], sems.at[at]))
    return copies


def stage_rows(stage, own_ref, recv_ref, image):
    for row in range(OWN):
        stage[image, row, :SIDE, :] = own_ref[image, SHIFT + row]
    for row in range(SHIFT):
        stage[image, OWN + row, :SIDE, :] = recv_ref[image, row]


def to_windows(stage, perm, image):
    flat = stage[image].reshape(WIN * COLS, D)
    return nn(perm, flat)


def pad_rows(values):
    return jnp.concatenate([values, jnp.zeros((SEG - PAD, values.shape[1]), f32)], axis=0)


def head_masks(dtype):
    lane = lax.broadcasted_iota(jnp.int32, (SEG, LANES), 1) // HEAD
    return [jnp.where(lane == head, 1.0, 0.0).astype(dtype) for head in range(QUAD)]


def spread(block, masks):
    return jnp.concatenate([block * mask for mask in masks], axis=0)


def forward_attention(
    owners, own_ref, recv_ref, perm_ref, vec_ref, table_ref, *rest, shards, pics
):
    weight_refs = rest[:shards]
    xw_ref, qkv_ref, att_ref, weight, stage, proj, sems = rest[shards:]

    @pl.when(pl.program_id(0) == 0)
    def _():
        copies = load_shards(owners, weight_refs, weight, sems)
        for copy in copies:
            copy.start()
        stage[...] = jnp.zeros_like(stage)
        for copy in copies:
            copy.wait()

    perm = perm_ref[...]
    gain = vec_ref[0:1]
    beta = vec_ref[1:2]
    qb = vec_ref[2:3]
    vb = vec_ref[3:4]
    for image in range(pics):
        stage_rows(stage, own_ref, recv_ref, image)
        values = to_windows(stage, perm, image)
        rows = pl.ds(image * PIC, PIC)
        xw_ref[rows] = values.astype(bf16)
        hat, _ = stats(values)
        normed = (hat * gain + beta).astype(bf16)
        proj[rows, 0:D] = ((nn(normed, weight[:, 0:D]) + qb) * SCALE)
        proj[rows, D : 2 * D] = nn(normed, weight[:, D : 2 * D])
        proj[rows, 2 * D :] = nn(normed, weight[:, 2 * D :]) + vb
    qkv_ref[...] = proj[...].astype(bf16)

    masks = head_masks(bf16)
    half = lax.broadcasted_iota(jnp.int32, (PAD, LANES), 1) < SEG
    row_head = lax.broadcasted_iota(jnp.int32, (QUAD * SEG, LANES), 0) // SEG
    lane_head = lax.broadcasted_iota(jnp.int32, (QUAD * SEG, LANES), 1) // HEAD
    ones = jnp.where(row_head == lane_head, 1.0, 0.0).astype(bf16)

    def image_step(image, carry):
        for window in range(2):
            start = pl.multiple_of(image * PIC + window * PAD, 8)
            rows = pl.ds(start, PAD)
            for group in range(GROUPS):
                at = group * LANES
                query = pad_rows(proj[rows, at : at + LANES]).astype(bf16)
                key = pad_rows(proj[rows, D + at : D + at + LANES]).astype(bf16)
                value = pad_rows(proj[rows, 2 * D + at : 2 * D + at + LANES]).astype(bf16)
                scores = nt(query, spread(key, masks))[:PAD] + table_ref[window, group]
                parts = []
                for side in range(2):
                    block = scores[:, side * LANES : (side + 1) * LANES]
                    low = jnp.max(jnp.where(half, block, NEGATIVE), -1, keepdims=True)
                    high = jnp.max(jnp.where(half, NEGATIVE, block), -1, keepdims=True)
                    parts.append(jnp.exp(block - jnp.where(half, low, high)))
                probs = pad_rows(jnp.concatenate(parts, axis=1)).astype(bf16)
                right = jnp.concatenate([spread(value, masks), ones], axis=1)
                both = nn(probs, right)[:PAD]
                mixed = both[:, :LANES] / both[:, LANES:]
                att_ref[rows, at : at + LANES] = mixed.astype(bf16)
        return carry

    lax.fori_loop(0, pics, image_step, 0)


def middle(
    owners, used, own_ref, recv_ref, xw_ref, att_ref, perm_ref, back_ref, vec_ref, upb_ref,
    *rest, shards, pics
):
    out_refs = rest[: 3 * shards]
    wo_refs, w1_refs, w2_refs = out_refs[:shards], out_refs[shards : 2 * shards], out_refs[2 * shards :]
    (
        keep_ref, send_ref, resid_ref, datt_ref, gw1_ref, gw2_ref, gwo_ref, vecg_ref, upg_ref,
        wo, w1, w2, stage, n2s, cts, gn2s, mlps, acc1, acc2, acco, sems,
    ) = rest[3 * shards :]
    step = pl.program_id(0)
    last = pl.num_programs(0) - 1

    @pl.when(step == 0)
    def _():
        copies = (
            load_shards(owners, wo_refs, wo, sems.at[0])
            + load_shards(owners, w1_refs, w1, sems.at[1])
            + load_shards(owners, w2_refs, w2, sems.at[2])
        )
        for copy in copies:
            copy.start()
        stage[...] = jnp.zeros_like(stage)
        acc1[...] = jnp.zeros_like(acc1)
        acc2[...] = jnp.zeros_like(acc2)
        acco[...] = jnp.zeros_like(acco)
        vecg_ref[...] = jnp.zeros_like(vecg_ref)
        upg_ref[...] = jnp.zeros_like(upg_ref)
        for copy in copies:
            copy.wait()

    perm = perm_ref[...]
    back = back_ref[...]
    pbias = vec_ref[4:5]
    gain = vec_ref[5:6]
    beta = vec_ref[6:7]
    dbias = vec_ref[7:8]
    rows_all = pics * PIC
    for image in range(pics):
        stage_rows(stage, own_ref, recv_ref, image)
        flag = used[step * pics + image].astype(f32)
        rows = pl.ds(image * PIC, PIC)
        cts[rows] = (to_windows(stage, perm, image) * flag).astype(bf16)
    proj = (nn(att_ref[...], wo[...]) + pbias).astype(bf16)
    resid = xw_ref[...].astype(f32) + proj.astype(f32)
    hat, rstd = stats(resid)
    n2s[...] = (hat * gain + beta).astype(bf16)
    mlps[...] = resid + dbias
    gn2s[...] = jnp.zeros_like(gn2s)
    n2t = n2s[...].T
    ctt = cts[...].T
    span = w1.shape[1] // 4

    def chunk(index, carry):
        cols = pl.ds(pl.multiple_of(index * span, span), span)
        pre = nn(n2s[...], w1[:, cols]) + upb_ref[0:1, cols]
        dact = nt(cts[...], w2[cols, :])
        phi = 0.5 * (1.0 + lax.erf(pre * 0.7071067811865476))
        act = (pre * phi).astype(bf16)
        slope = phi + pre * jnp.exp(-0.5 * pre * pre) * 0.3989422804014327
        gpre = dact * slope
        upg_ref[0:1, cols] += rowsum(gpre)
        hidden = gpre.astype(bf16)
        mlps[...] += nn(act, w2[cols, :])
        gn2s[...] += nt(hidden, w1[:, cols])
        acc2[:, cols] += nn(ctt, act)
        acc1[:, cols] += nn(n2t, hidden)
        return carry

    lax.fori_loop(0, 4, chunk, 0)

    gn2 = gn2s[...]
    ct = cts[...].astype(f32)
    gresid = ct + norm_back(gn2 * gain, hat, rstd)
    vecg_ref[4:5] += rowsum(gresid)
    vecg_ref[5:6] += rowsum(gn2 * hat)
    vecg_ref[6:7] += rowsum(gn2)
    vecg_ref[7:8] += rowsum(ct)
    low = gresid.astype(bf16)
    resid_ref[...] = low
    datt_ref[...] = nt(low, wo[...]).astype(bf16)
    acco[...] += tn(att_ref[...], low)
    for image in range(pics):
        flag = used[step * pics + image].astype(f32)
        rows = pl.ds(image * PIC, PIC)
        mine = (mlps[rows] * flag).astype(bf16)
        framed = nn(back, mine).astype(bf16).reshape(WIN, COLS, D)
        for row in range(OWN):
            keep_ref[image, SHIFT + row] = framed[row, :SIDE]
        for row in range(SHIFT):
            keep_ref[image, row] = framed[OWN + row, :SIDE]
            send_ref[image, row] = framed[OWN + row, :SIDE]

    @pl.when(step == last)
    def _():
        gwo_ref[...] = acco[...].astype(bf16)
        gw1_ref[...] = acc1[...].astype(bf16)
        for piece in range(4):
            cols = slice(piece * span, (piece + 1) * span)
            gw2_ref[cols, :] = acc2[:, cols].T.astype(bf16)


def backward_attention(
    owners, xw_ref, qkv_ref, resid_ref, datt_ref, back_ref, vec_ref, table_ref,
    *rest, shards, pics
):
    weight_refs = rest[:shards]
    (
        keep_ref, send_ref, gw_ref, vecg_ref, tab_ref, weight, dqkv, acc, sems,
    ) = rest[shards:]
    step = pl.program_id(0)
    last = pl.num_programs(0) - 1

    @pl.when(step == 0)
    def _():
        copies = load_shards(owners, weight_refs, weight, sems)
        for copy in copies:
            copy.start()
        acc[...] = jnp.zeros_like(acc)
        vecg_ref[...] = jnp.zeros_like(vecg_ref)
        tab_ref[...] = jnp.zeros_like(tab_ref)
        for copy in copies:
            copy.wait()

    masks = head_masks(bf16)
    picks = head_masks(f32)

    def image_step(image, carry):
        for window in range(2):
            start = pl.multiple_of(image * PIC + window * PAD, 8)
            rows = pl.ds(start, PAD)
            for group in range(GROUPS):
                at = group * LANES
                query = pad_rows(qkv_ref[rows, at : at + LANES].astype(f32)).astype(bf16)
                key = pad_rows(qkv_ref[rows, D + at : D + at + LANES].astype(f32)).astype(bf16)
                value = pad_rows(
                    qkv_ref[rows, 2 * D + at : 2 * D + at + LANES].astype(f32)
                ).astype(bf16)
                datt = pad_rows(datt_ref[rows, at : at + LANES].astype(f32)).astype(bf16)
                queries = spread(query, masks)
                datts = spread(datt, masks)
                scores = nt(key, queries)[:PAD] + table_ref[window, group]
                shifted = jnp.exp(scores - jnp.max(scores, 0, keepdims=True))
                probs = shifted * (1.0 / jnp.sum(shifted, 0, keepdims=True))
                dprobs = nt(value, datts)[:PAD]
                inner = jnp.sum(probs * dprobs, 0, keepdims=True)
                dscores = probs * (dprobs - inner)
                tab_ref[group] += dscores
                dlow = pad_rows(dscores).astype(bf16)
                plow = pad_rows(probs).astype(bf16)
                dkey = nn(dlow, queries)[:PAD]
                dvalue = nn(plow, datts)[:PAD]
                tall = tn(dlow, key)
                dquery = tall[0:PAD] * picks[0][:PAD]
                for head in range(1, QUAD):
                    dquery += tall[head * SEG : head * SEG + PAD] * picks[head][:PAD]
                dqkv[rows, at : at + LANES] = dquery * SCALE
                dqkv[rows, D + at : D + at + LANES] = dkey
                dqkv[rows, 2 * D + at : 2 * D + at + LANES] = dvalue
        return carry

    lax.fori_loop(0, pics, image_step, 0)

    gain = vec_ref[0:1]
    beta = vec_ref[1:2]
    hat, rstd = stats(xw_ref[...].astype(f32))
    normed = (hat * gain + beta).astype(bf16)
    vecg_ref[2:3] += rowsum(dqkv[:, 0:D])
    vecg_ref[3:4] += rowsum(dqkv[:, 2 * D :])
    low = dqkv[...].astype(bf16)
    acc[...] += tn(normed, low)
    gnormed = nt(low, weight[...]).astype(bf16).astype(f32)
    vecg_ref[0:1] += rowsum(gnormed * hat)
    vecg_ref[1:2] += rowsum(gnormed)
    ginput = resid_ref[...].astype(f32) + norm_back(gnormed * gain, hat, rstd)
    glow = ginput.astype(bf16)
    back = back_ref[...]
    for image in range(pics):
        framed = nn(back, glow[image * PIC : (image + 1) * PIC]).reshape(WIN, COLS, D)
        for row in range(OWN):
            keep_ref[image, SHIFT + row] = framed[row, :SIDE]
        for row in range(SHIFT):
            keep_ref[image, row] = framed[OWN + row, :SIDE]
            send_ref[image, row] = framed[OWN + row, :SIDE].astype(bf16)

    @pl.when(step == last)
    def _():
        gw_ref[...] = acc[...].astype(bf16)


def gather(piece):
    held = [piece]
    for bit in reversed(range(bits_of("fsdp"))):
        held = held + [partner(one, "fsdp", bit) for one in held]
    return held


def held_masks():
    masks = [0]
    for bit in reversed(range(bits_of("fsdp"))):
        masks = masks + [mask | (1 << bit) for mask in masks]
    return masks


def in_order(held, me):
    masks = held_masks()
    count = len(held)
    table = [None] * count
    for mask, piece in zip(masks, held):
        table[mask] = piece
    stacked = jnp.stack(table)
    for bit in range(bits_of("fsdp")):
        split = stacked.reshape(count >> (bit + 1), 2, 1 << bit, *stacked.shape[1:])
        swap = (me >> bit) & 1
        split = jnp.where(swap == 1, split[:, ::-1], split)
        stacked = split.reshape(stacked.shape)
    return stacked


def reduce_owned(grad, me):
    ranks = lax.axis_size("fsdp")
    own = grad.reshape(ranks, grad.shape[0] // ranks, grad.shape[1])
    for bit in range(bits_of("fsdp")):
        pairs = own.reshape(own.shape[0] // 2, 2, *own.shape[1:])
        mine = (me >> bit) & 1
        keep = lax.dynamic_index_in_dim(pairs, mine, 1, keepdims=False)
        send = lax.dynamic_index_in_dim(pairs, 1 - mine, 1, keepdims=False)
        got = partner(send, "fsdp", bit)
        own = (keep.astype(f32) + got.astype(f32)).astype(bf16)
    own = own[0]
    for axis in ("band", "img"):
        for bit in range(bits_of(axis)):
            own = (own.astype(f32) + partner(own, axis, bit).astype(f32)).astype(bf16)
    return own.astype(f32)


def reduce_small(flat):
    for axis in ("fsdp", "band", "img"):
        for bit in range(bits_of(axis)):
            flat = flat + partner(flat, axis, bit)
    return flat


def window_tables(table):
    places = jnp.arange(PAD)
    other = jnp.arange(SEG)
    rowq, colq = places // WIN, places % WIN
    rowk, colk = other // WIN, other % WIN
    index = (rowq[:, None] - rowk[None, :] + WIN - 1) * (2 * WIN - 1) + (
        colq[:, None] - colk[None, :] + WIN - 1
    )
    real = (places[:, None] < LEN) & (other[None, :] < LEN)
    index = jnp.where(real, index, TABLE)
    flip = (rowk[None, :] - rowq[:, None] + WIN - 1) * (2 * WIN - 1) + (
        colk[None, :] - colq[:, None] + WIN - 1
    )
    flip = jnp.where(real, flip, TABLE)
    one = (index[..., None] == jnp.arange(TABLE)).astype(bf16)
    two = (flip[..., None] == jnp.arange(TABLE)).astype(bf16)
    return one, two


def regions(band):
    cells = jnp.arange(SIDE)
    region = jnp.where(cells < SIDE - WIN, 0, jnp.where(cells < SIDE - SHIFT, 1, 2))
    rows = lax.dynamic_slice_in_dim(region, band * WIN, WIN)
    cols = region.reshape(SIDE // WIN, WIN)
    label = rows[None, :, None] * 3 + cols[:, None, :]
    return label.reshape(SIDE // WIN, LEN)


def shards(
    block_input,
    slot_used,
    cotangent,
    ln1_gain,
    ln1_bias,
    w_qkv,
    q_bias,
    v_bias,
    rel_table,
    w_out,
    out_bias,
    ln2_gain,
    ln2_bias,
    w_fc1,
    fc1_bias,
    w_fc2,
    fc2_bias,
):
    slots = block_input.shape[0]
    pics = 4
    steps = slots // pics
    rows = pics * PIC
    ranks = lax.axis_size("fsdp")
    width = w_fc1.shape[1]
    me = lax.axis_index("fsdp")
    band = lax.axis_index("band")
    owners = jnp.stack([me ^ mask for mask in held_masks()]).astype(jnp.int32)

    held_qkv = gather(w_qkv)
    pieces = (
        ln1_gain, ln1_bias, q_bias, v_bias, out_bias, ln2_gain, ln2_bias, fc2_bias,
        fc1_bias, rel_table.reshape(-1),
    )
    small = in_order(gather(jnp.concatenate(pieces)), me)
    arrived = partner(block_input[:, :SHIFT], "band", 0)
    per = ln1_gain.shape[0]
    vectors = small[:, : 8 * per].reshape(ranks, 8, per).transpose(1, 0, 2).reshape(8, D).astype(f32)
    ups = fc1_bias.shape[0]
    up_bias = small[:, 8 * per : 8 * per + ups].reshape(1, width).astype(f32)
    table = small[:, 8 * per + ups :].reshape(HEADS, TABLE)

    later = lax.optimization_barrier((w_out, w_fc1, w_fc2, cotangent[:, :SHIFT], held_qkv[-1], arrived))
    held_out = gather(later[0])
    held_up = gather(later[1])
    held_down = gather(later[2])
    ct_arrived = partner(later[3], "band", 0)

    one, two = window_tables(table)
    label = regions(band)
    label_q = jnp.pad(label, ((0, 0), (0, PAD - LEN)), constant_values=-1)
    label_k = jnp.pad(label, ((0, 0), (0, SEG - LEN)), constant_values=-1)
    differ = label_q[:, :, None] != label_k[:, None, :]
    spot = jnp.arange(SEG)
    block_f = jnp.where(differ | (spot[None, None, :] >= LEN), NEGATIVE, 0.0).astype(f32)
    block_b = jnp.where(
        (differ & (spot[None, None, :] < LEN)) | (jnp.arange(PAD)[None, :, None] >= LEN), NEGATIVE, 0.0
    ).astype(f32)
    quads = table.reshape(GROUPS, QUAD, TABLE)
    bias_f = jnp.einsum("ght,ijt->gihj", quads, one, preferred_element_type=f32)
    bias_b = jnp.einsum("ght,ijt->gihj", quads, two, preferred_element_type=f32)
    table_f = (bias_f[None] + block_f[:, None, :, None, :]).reshape(2, GROUPS, PAD, QUAD * SEG)
    table_b = (bias_b[None] + block_b[:, None, :, None, :]).reshape(2, GROUPS, PAD, QUAD * SEG)

    target = jnp.arange(PIC)
    window, spot_in = target // PAD, target % PAD
    source = (spot_in // WIN) * COLS + (window * WIN + spot_in % WIN + SHIFT) % SIDE
    source = jnp.where(spot_in < LEN, source, -1)
    perm = (source[:, None] == jnp.arange(WIN * COLS)[None, :]).astype(bf16)
    back = (source[None, :] == jnp.arange(WIN * COLS)[:, None]).astype(bf16)

    any_spec = pl.BlockSpec(memory_space=pl.ANY)

    def whole(shape):
        return pl.BlockSpec(shape, lambda i, *_: (0,) * len(shape))

    pic_spec = pl.BlockSpec((pics, WIN, SIDE, D), lambda i, *_: (i, 0, 0, 0))
    arr_spec = pl.BlockSpec((pics, SHIFT, SIDE, D), lambda i, *_: (i, 0, 0, 0))

    def row_spec(cols):
        return pl.BlockSpec((rows, cols), lambda i, *_: (i, 0))

    total = slots * PIC
    params = pltpu.CompilerParams(
        dimension_semantics=("arbitrary",), vmem_limit_bytes=60 * 1024 * 1024
    )

    xw, qkv, att = pl.pallas_call(
        functools.partial(forward_attention, shards=ranks, pics=pics),
        grid_spec=pltpu.PrefetchScalarGridSpec(
            num_scalar_prefetch=1,
            grid=(steps,),
            in_specs=[
                pic_spec, arr_spec, whole((PIC, PIC)), whole((8, D)),
                whole((2, GROUPS, PAD, QUAD * SEG)),
            ] + [any_spec] * ranks,
            out_specs=[row_spec(D), row_spec(3 * D), row_spec(D)],
            scratch_shapes=[
                pltpu.VMEM((D, 3 * D), bf16),
                pltpu.VMEM((pics, WIN, COLS, D), bf16),
                pltpu.VMEM((rows, 3 * D), f32),
                pltpu.SemaphoreType.DMA((ranks,)),
            ],
        ),
        out_shape=[
            jax.ShapeDtypeStruct((total, D), bf16),
            jax.ShapeDtypeStruct((total, 3 * D), bf16),
            jax.ShapeDtypeStruct((total, D), bf16),
        ],
        compiler_params=params,
        name="attention_forward",
    )(owners, block_input, arrived, perm, vectors, table_f, *held_qkv)

    keep, send, resid, datt, gw1, gw2, gwo, vecg, upg = pl.pallas_call(
        functools.partial(middle, shards=ranks, pics=pics),
        grid_spec=pltpu.PrefetchScalarGridSpec(
            num_scalar_prefetch=2,
            grid=(steps,),
            in_specs=[
                pic_spec, arr_spec, row_spec(D), row_spec(D), whole((PIC, PIC)),
                whole((PIC, PIC)), whole((8, D)), whole((1, width)),
            ] + [any_spec] * (3 * ranks),
            out_specs=[
                pic_spec, arr_spec, row_spec(D), row_spec(D), whole((D, width)),
                whole((width, D)), whole((D, D)), whole((8, D)), whole((1, width)),
            ],
            scratch_shapes=[
                pltpu.VMEM((D, D), bf16),
                pltpu.VMEM((D, width), bf16),
                pltpu.VMEM((width, D), bf16),
                pltpu.VMEM((pics, WIN, COLS, D), bf16),
                pltpu.VMEM((rows, D), bf16),
                pltpu.VMEM((rows, D), bf16),
                pltpu.VMEM((rows, D), f32),
                pltpu.VMEM((rows, D), f32),
                pltpu.VMEM((D, width), f32),
                pltpu.VMEM((D, width), f32),
                pltpu.VMEM((D, D), f32),
                pltpu.SemaphoreType.DMA((3, ranks)),
            ],
        ),
        out_shape=[
            jax.ShapeDtypeStruct((slots, WIN, SIDE, D), bf16),
            jax.ShapeDtypeStruct((slots, SHIFT, SIDE, D), bf16),
            jax.ShapeDtypeStruct((total, D), bf16),
            jax.ShapeDtypeStruct((total, D), bf16),
            jax.ShapeDtypeStruct((D, width), bf16),
            jax.ShapeDtypeStruct((width, D), bf16),
            jax.ShapeDtypeStruct((D, D), bf16),
            jax.ShapeDtypeStruct((8, D), f32),
            jax.ShapeDtypeStruct((1, width), f32),
        ],
        compiler_params=params,
        name="mlp_both",
    )(
        owners, slot_used.reshape(-1), cotangent, ct_arrived, xw, att, perm, back, vectors, up_bias,
        *held_out, *held_up, *held_down,
    )
    output = lax.dynamic_update_slice(keep, partner(send, "band", 0), (0, 0, 0, 0))

    gkeep, gsend, gwq, vecg1, tab = pl.pallas_call(
        functools.partial(backward_attention, shards=ranks, pics=pics),
        grid_spec=pltpu.PrefetchScalarGridSpec(
            num_scalar_prefetch=1,
            grid=(steps,),
            in_specs=[
                row_spec(D), row_spec(3 * D), row_spec(D), row_spec(D), whole((PIC, PIC)),
                whole((8, D)), whole((2, GROUPS, PAD, QUAD * SEG)),
            ] + [any_spec] * ranks,
            out_specs=[
                pic_spec, arr_spec, whole((D, 3 * D)), whole((8, D)),
                whole((GROUPS, PAD, QUAD * SEG)),
            ],
            scratch_shapes=[
                pltpu.VMEM((D, 3 * D), bf16),
                pltpu.VMEM((rows, 3 * D), f32),
                pltpu.VMEM((D, 3 * D), f32),
                pltpu.SemaphoreType.DMA((ranks,)),
            ],
        ),
        out_shape=[
            jax.ShapeDtypeStruct((slots, WIN, SIDE, D), f32),
            jax.ShapeDtypeStruct((slots, SHIFT, SIDE, D), bf16),
            jax.ShapeDtypeStruct((D, 3 * D), bf16),
            jax.ShapeDtypeStruct((8, D), f32),
            jax.ShapeDtypeStruct((GROUPS, PAD, QUAD * SEG), f32),
        ],
        compiler_params=params,
        name="attention_backward",
    )(owners, xw, qkv, resid, datt, back, vectors, table_b, *held_qkv)
    grad_input = lax.dynamic_update_slice(
        gkeep, partner(gsend, "band", 0).astype(f32), (0, 0, 0, 0)
    )

    own_up = reduce_owned(gw1, me)
    own_down = reduce_owned(gw2, me)
    own_out = reduce_owned(gwo, me)
    own_qkv = reduce_owned(gwq, me)
    spots = tab.reshape(GROUPS, PAD, QUAD, SEG)
    grad_table = jnp.einsum(
        "gihj,ijt->ght", spots, two.astype(f32), precision=lax.Precision.HIGHEST
    )
    flat = reduce_small(
        jnp.concatenate([vecg1[:4].reshape(-1), vecg[4:].reshape(-1), upg.reshape(-1), grad_table.reshape(-1)])
    )
    lanes = flat[: 8 * D].reshape(8, ranks, per)
    mine = lax.dynamic_index_in_dim(lanes, me, 1, keepdims=False)
    own_upb = lax.dynamic_slice_in_dim(flat, 8 * D + me * ups, ups)
    heads = rel_table.shape[0]
    own_table = lax.dynamic_slice_in_dim(flat, 8 * D + width + me * heads * TABLE, heads * TABLE)
    return (
        output,
        grad_input,
        mine[0],
        mine[1],
        own_qkv,
        mine[2],
        mine[3],
        own_table.reshape(heads, TABLE),
        own_out,
        mine[4],
        mine[5],
        mine[6],
        own_up,
        own_upb,
        own_down,
        mine[7],
    )


def solution(mesh):
    pictures = P(("img", "fsdp"), "band", None, None)
    flat = P("fsdp")
    wide = P("fsdp", None)
    return jax.shard_map(
        shards,
        mesh=mesh,
        in_specs=(
            pictures, P(("img", "fsdp"), None), pictures, flat, flat, wide, flat, flat, wide, wide,
            flat, flat, flat, wide, flat, wide, flat,
        ),
        out_specs=(
            pictures, pictures, flat, flat, wide, flat, flat, wide, wide, flat, flat, flat, wide,
            flat, wide, flat,
        ),
        check_vma=False,
    )
```

time: 901 us -> 453 us (0.50)
  matrix products: 243 us -> 5.12 us
  local copies, waits for them, and re-layouts: 300 us -> 63.4 us
  Pallas kernels: 0 us -> 172 us
  blocking collectives: 110 us -> 0 us
  other arithmetic: 90.6 us -> 16.6 us
  starting transfers between devices: 6.11 us -> 42.3 us
  waiting for transfers between devices: 123 us -> 151 us
  between operations: 17.6 us -> 1.31 us
    dot_general x20 -> x3, matrix products: 243 us -> 5.12 us  [the longest x1 1.88 us: shards(): bias_f = jnp.einsum('ght,ijt->gihj', quads, one, preferred_element_type=f32)]
    pallas_call x0 -> x3, Pallas kernels: none -> 172 us  [the longest x1 73 us: shards(): pl.pallas_call(functools.partial(backward_attention, shards=ranks, pics=p...]
    reshape x22 -> x6, local copies, waits for them, and re-layouts: 172 us -> 2.89 us  [the longest x1 1.15 us: shards(): spots = tab.reshape(GROUPS, PAD, QUAD, SEG)]
    ppermute x4 -> x44, waiting for transfers between devices: 23.3 us -> 151 us  [partner(): return lax.ppermute(value, axis, pairs)]
    reduce_scatter x4 -> x0, waiting for transfers between devices: 62.4 us -> none  [the longest x1 47.1 us: shards(): lax.psum_scatter(s11, 'fsdp', scatter_dimension=0, tiled=True)]
    all_gather x11 -> x0, blocking collectives: 60.9 us -> none  [the longest x1 7.86 us: shards(): lax.all_gather(w_out, 'fsdp', axis=0, tiled=True)]
    reduce_sum x10 -> x0, other arithmetic: 59.5 us -> none  [the longest x1 21.2 us: shards(): jnp.sum(grad_scores, 0).reshape(HEADS, length * length)]
    convert_element_type x7 -> x0, local copies, waits for them, and re-layouts: 40.7 us -> none  [the longest x2 11.6 us: shards(): resid = inputs + restored.astype(f32).reshape(-1, D)]
  transfers between devices with their start and end apart: 12 -> 44, of which waited for: 4 -> 17; matrix products, arithmetic and copies ran while one was open for 51% -> 14% of each run, Pallas kernels for 0% -> 8%
where the time goes in v1:
time: 453 us; the launch traced here: 451 us
  Pallas kernels  172 us (38%)
  waiting for transfers between devices  151 us (33%)
  local copies, waits for them, and re-layouts  63.4 us (14%)
  starting transfers between devices  42.3 us (9%)
  other arithmetic  16.6 us (4%)
  matrix products  5.12 us (1%)
    ppermute x44, waiting for transfers between devices, partner(): return lax.ppermute(value, axis, pairs)  151 us
    pallas_call x1, Pallas kernels, shards(): pl.pallas_call(functools.partial(backward_attention, shards=ranks, pics=p...  73 us
    pallas_call x1, Pallas kernels, shards(): pl.pallas_call(functools.partial(middle, shards=ranks, pics=pics), grid_s...  64.5 us
    ppermute x44, starting transfers between devices, partner(): return lax.ppermute(value, axis, pairs)  42.3 us
    pallas_call x1, Pallas kernels, shards(): pl.pallas_call(functools.partial(forward_attention, shards=ranks, pics=pi...  34.4 us
    unnamed x65, local copies, waits for them, and re-layouts  32.4 us
  transfers between devices with their start and end apart: 44, of which 17 were waited for; matrix products, arithmetic and copies ran while one was open for 14% of the time, Pallas kernels for 8%

profile of v1, /device:TPU:0, one launch (start us, length us, event | category | flops | bytes accessed | tf_op | source)
XLA Modules:
  0.0 451.5 jit_solution(13554066591085854070)
XLA Ops:
  15.9 3.0 collective-permute-start.5
  19.4 2.2 slice.57
  27.2 2.4 copy.74.own_ref
  29.8 2.4 copy.76.own_ref
  37.4 9.5 %collective-permute-done.2 = bf16[24,3,14,512]{3,0,2,1:T(8,128)(2,1)} collective-permute-done((bf16[24,3,14,512]{3,0,2,1:T(8,128)(2,1)}, bf16[24,3,14,512]{3,0,2,1:T(8,128)(2,1)}, u32[]{:S(2)}, u32[]{:S(2)}) %collective-permute-start.2) | collective-permute-done | bytes 1032224 | tf_op jit(solution)/shard_map/ppermute | solution.py:38
  46.9 1.8 collective-permute-start.11
  50.7 1.9 fusion.18
  52.6 1.9 fusion.15
  56.7 17.6 %collective-permute-done.8.rest_1_ = bf16[128,512]{1,0:T(8,128)(2,1)S(1)} collective-permute-done((bf16[128,512]{1,0:T(8,128)(2,1)S(1)}, bf16[128,512]{1,0:T(8,128)(2,1)S(1)}, u32[]{:S(2)}, u32[]{:S(2)}) %collective-permute-start.8) | collective-permute-done | bytes 131104 | tf_op jit(solution)/shard_map/ppermute | solution.py:38
  83.1 2.6 copy.75.recv_ref
  85.6 34.4 %attention_forward.1 = (bf16[2688,512]{1,0:T(8,128)(2,1)}, bf16[2688,1536]{1,0:T(8,128)(2,1)}, bf16[2688,512]{1,0:T(8,128)(2,1)}) custom-call(s32[4]{0:T(128)} %pad_add_fusion.owners, bf16[24,7,14,512]{3,2,1,0:T(8,128)(2,1)} %copy.74.own_ref, bf16[24,3,14,512]{3,2,1,0:T(8,128)(2,1)} %copy.75.recv_ref, bf16[112,112]{1,0:T(8,128)(2,1)} %get-tuple-element.135.perm_ref, ...), custom_call_target="tpu_custom_call" | custom-call | tf_op jit(solution)/shard_map/attention_forward/pallas_call | solution.py:531
  120.0 2.6 copy.77.recv_ref
  123.3 64.5 %mlp_both.1 = (bf16[24,7,14,512]{3,2,1,0:T(8,128)(2,1)}, bf16[24,3,14,512]{3,2,1,0:T(8,128)(2,1)}, bf16[2688,512]{1,0:T(8,128)(2,1)}, bf16[2688,512]{1,0:T(8,128...) custom-call(s32[4]{0:T(128)} %pad_add_fusion.owners, ...), custom_call_target="tpu_custom_call" | custom-call | tf_op jit(solution)/shard_map/mlp_both/pallas_call | solution.py:557
  187.8 73.0 %attention_backward.1 = (f32[24,7,14,512]{3,2,1,0:T(8,128)}, bf16[24,3,14,512]{3,2,1,0:T(8,128)(2,1)}, bf16[512,1536]{1,0:T(8,128)(2,1)}, f32[8,512]{1,0:T(8,128)}, f32[4,56,256]{2,1,0:T(8,128)}) custom-call(s32[4]{0:T(128)} %pad_add_fusion.owners, bf16[2688,512]{1,0:T(8,128)(2,1)} %get-tuple-element.38.xw_ref, ...), custom_call_target="tpu_custom_call" | custom-call | tf_op jit(solution)/shard_map/attention_backward/pallas_call | solution.py:604
  267.4 2.2 collective-permute-done.20
  276.9 2.1 dynamic-slice_bitcast_fusion.2
  279.0 2.8 collective-permute-start.23
  291.7 2.3 collective-permute-start.33
  295.7 5.1 %collective-permute-done.33 = bf16[128,512]{1,0:T(8,128)(2,1)S(1)} collective-permute-done((bf16[128,512]{1,0:T(8,128)(2,1)S(1)}, bf16[128,512]{1,0:T(8,128)(2,1)S(1)}, u32[]{:S(2)}, u32[]{:S(2)}) %collective-permute-start.33) | collective-permute-done | bytes 131104 | tf_op jit(solution)/shard_map/ppermute | solution.py:38
  303.0 10.6 %collective-permute-done.18 = bf16[24,3,14,512]{3,0,2,1:T(8,128)(2,1)} collective-permute-done((bf16[24,3,14,512]{3,0,2,1:T(8,128)(2,1)}, bf16[24,3,14,512]{3,0,2,1:T(8,128)(2,1)}, u32[]{:S(2)}, u32[]{:S(2)}) %collective-permute-start.18) | collective-permute-done | bytes 1032224 | tf_op jit(solution)/shard_map/ppermute | solution.py:38
  315.1 2.6 copy_dynamic-update-slice_fusion
  317.7 7.7 %copy.88 = f32[24,7,14,512]{3,0,2,1:T(8,128)} copy(f32[24,7,14,512]{3,2,1,0:T(8,128)} %copy_dynamic-update-slice_fusion) | data formatting | bytes 9633792
  325.4 9.7 %collective-permute-done.17 = bf16[24,3,14,512]{3,0,2,1:T(8,128)(2,1)S(1)} collective-permute-done((bf16[24,3,14,512]{3,0,2,1:T(8,128)(2,1)}, bf16[24,3,14,512]{3,0,2,1:T(8,128)(2,1)S(1)}, u32[]{:S(2)}, u32[]{:S(2)}) %collective-permute-start.17) | collective-permute-done | bytes 1032224 | tf_op jit(solution)/shard_map/ppermute | solution.py:38
  335.5 2.8 copy.87
  345.4 9.4 %collective-permute-done.40 = bf16[1,512,512]{2,1,0:T(8,128)(2,1)S(1)} collective-permute-done((bf16[1,512,512]{2,1,0:T(8,128)(2,1)S(1)}, bf16[1,512,512]{2,1,0:T(8,128)(2,1)S(1)}, u32[]{:S(2)}, u32[]{:S(2)}) %collective-permute-start.40) | collective-permute-done | bytes 524320 | tf_op jit(solution)/shard_map/ppermute | solution.py:38
  356.5 8.2 %collective-permute-done.35 = bf16[1,128,2048]{2,1,0:T(8,128)(2,1)S(1)} collective-permute-done((bf16[1,128,2048]{2,1,0:T(8,128)(2,1)S(1)}, bf16[1,128,2048]{2,1,0:T(8,128)(2,1)S(1)}, u32[]{:S(2)}, u32[]{:S(2)}) %collective-permute-start.35) | collective-permute-done | bytes 524320 | tf_op jit(solution)/shard_map/ppermute | solution.py:38
  368.8 8.7 %collective-permute-done.36 = bf16[128,2048]{1,0:T(8,128)(2,1)S(1)} collective-permute-done((bf16[128,2048]{1,0:T(8,128)(2,1)S(1)}, bf16[128,2048]{1,0:T(8,128)(2,1)S(1)}, u32[]{:S(2)}, u32[]{:S(2)}) %collective-permute-start.36) | collective-permute-done | bytes 524320 | tf_op jit(solution)/shard_map/ppermute | solution.py:38
  378.7 2.2 collective-permute-start.28
  380.9 18.4 %collective-permute-done.42 = bf16[512,512]{1,0:T(8,128)(2,1)S(1)} collective-permute-done((bf16[512,512]{1,0:T(8,128)(2,1)S(1)}, bf16[512,512]{1,0:T(8,128)(2,1)S(1)}, u32[]{:S(2)}, u32[]{:S(2)}) %collective-permute-start.42) | collective-permute-done | bytes 524320 | tf_op jit(solution)/shard_map/ppermute | solution.py:38
  399.6 9.9 %collective-permute-done.37 = bf16[128,2048]{1,0:T(8,128)(2,1)S(1)} collective-permute-done((bf16[128,2048]{1,0:T(8,128)(2,1)S(1)}, bf16[128,2048]{1,0:T(8,128)(2,1)S(1)}, u32[]{:S(2)}, u32[]{:S(2)}) %collective-permute-start.37) | collective-permute-done | bytes 524320 | tf_op jit(solution)/shard_map/ppermute | solution.py:38
  410.7 30.9 %collective-permute-done.43 = bf16[512,512]{1,0:T(8,128)(2,1)S(1)} collective-permute-done((bf16[512,512]{1,0:T(8,128)(2,1)S(1)}, bf16[512,512]{1,0:T(8,128)(2,1)S(1)}, u32[]{:S(2)}, u32[]{:S(2)}) %collective-permute-start.43) | collective-permute-done | bytes 524320 | tf_op jit(solution)/shard_map/ppermute | solution.py:38
  442.7 7.7 %collective-permute-done.38 = bf16[128,2048]{1,0:T(8,128)(2,1)S(1)} collective-permute-done((bf16[128,2048]{1,0:T(8,128)(2,1)S(1)}, bf16[128,2048]{1,0:T(8,128)(2,1)S(1)}, u32[]{:S(2)}, u32[]{:S(2)}) %collective-permute-start.38) | collective-permute-done | bytes 524320 | tf_op jit(solution)/shard_map/ppermute | solution.py:38
  (224 shorter events, 86.8 us)
Async XLA Ops:
  15.9 9.4 %collective-permute-start.5 = (bf16[2212]{0:T(1024)(128)(2,1)}, bf16[2212]{0:T(1024)(128)(2,1)}, u32[]{:S(2)}, u32[]{:S(2)}) collective-permute-start(bf16[2212]{0:T(1024)(128)(2,1)} %dynamic-update-slice.9), channel_id=1, source_target_pairs={{0,2},{1,3},{2,0},{3,1},{4,6},{5,7},{6,4},{7,5},{8,10},{9,11},{10,... | collective-permute-start | bytes 13280 | tf_op jit(solution)/shard_map/ppermute | solution.py:38
  18.9 14.5 %collective-permute-start.4 = (bf16[2212]{0:T(1024)(128)(2,1)}, bf16[2212]{0:T(1024)(128)(2,1)}, u32[]{:S(2)}, u32[]{:S(2)}) collective-permute-start(bf16[2212]{0:T(1024)(128)(2,1)} %dynamic-update-slice.9), channel_id=1, source_target_pairs={{0,1},{1,0},{2,3},{3,2},{4,5},{5,4},{6,7},{7,6},{8,9},{9,8},{10,11... | collective-permute-start | bytes 13280 | tf_op jit(solution)/shard_map/ppermute | solution.py:38
  18.9 16.6 %collective-permute-start = (bf16[128,1536]{1,0:T(8,128)(2,1)}, bf16[128,1536]{1,0:T(8,128)(2,1)S(1)}, u32[]{:S(2)}, u32[]{:S(2)}) collective-permute-start(bf16[128,1536]{1,0:T(8,128)(2,1)} %rest_0_.4), channel_id=1, source_target_pairs={{0,2},{1,3},{2,0},{3,1},{4,6},{5,7},{6,4},{7,5},{8,10},{9,11},{10,... | collective-permute-start | bytes 1179656 | tf_op jit(solution)/shard_map/ppermute | solution.py:38
  19.0 37.0 %collective-permute-start.7 = (bf16[128,1536]{1,0:T(8,128)(2,1)}, bf16[128,1536]{1,0:T(8,128)(2,1)S(1)}, u32[]{:S(2)}, u32[]{:S(2)}) collective-permute-start(bf16[128,1536]{1,0:T(8,128)(2,1)} %rest_0_.4), channel_id=1, source_target_pairs={{0,1},{1,0},{2,3},{3,2},{4,5},{5,4},{6,7},{7,6},{8,9},{9,8},{10,11... | collective-permute-start | bytes 1179656 | tf_op jit(solution)/shard_map/ppermute | solution.py:38
  21.7 25.3 %collective-permute-start.2 = (bf16[24,3,14,512]{3,0,2,1:T(8,128)(2,1)}, bf16[24,3,14,512]{3,0,2,1:T(8,128)(2,1)}, u32[]{:S(2)}, u32[]{:S(2)}) collective-permute-start(bf16[24,3,14,512]{3,0,2,1:T(8,128)(2,1)} %slice.57), channel_id=1, source_target_pairs={{0,16},{16,0},{1,17},{17,1},{2,18},{18,2},{3,19},{19,3},{4,20},{20... | collective-permute-start | bytes 3096584 | tf_op jit(solution)/shard_map/ppermute | solution.py:38
  46.9 27.8 %collective-permute-start.11 = (bf16[128,2048]{1,0:T(8,128)(2,1)S(1)}, bf16[128,2048]{1,0:T(8,128)(2,1)}, u32[]{:S(2)}, u32[]{:S(2)}) collective-permute-start(bf16[128,2048]{1,0:T(8,128)(2,1)S(1)} %copy-done.10), channel_id=1, source_target_pairs={{0,2},{1,3},{2,0},{3,1},{4,6},{5,7},{6,4},{7,5},{8,10},{9,11},{10,... | collective-permute-start | bytes 1572872 | tf_op jit(solution)/shard_map/ppermute | solution.py:38
  48.7 26.2 %collective-permute-start.14 = (bf16[512,512]{1,0:T(8,128)(2,1)}, bf16[512,512]{1,0:T(8,128)(2,1)}, u32[]{:S(2)}, u32[]{:S(2)}) collective-permute-start(bf16[512,512]{1,0:T(8,128)(2,1)} %rest_8_), channel_id=1, source_target_pairs={{0,2},{1,3},{2,0},{3,1},{4,6},{5,7},{6,4},{7,5},{8,10},{9,11},{10,... | collective-permute-start | bytes 1572872 | tf_op jit(solution)/shard_map/ppermute | solution.py:38
  49.0 33.1 %collective-permute-start.3 = (bf16[24,3,14,512]{3,0,2,1:T(8,128)(2,1)S(1)}, bf16[24,3,14,512]{3,0,2,1:T(8,128)(2,1)}, u32[]{:S(2)}, u32[]{:S(2)}) collective-permute-start(bf16[24,3,14,512]{3,0,2,1:T(8,128)(2,1)S(1)} %slice.56), channel_id=1, source_target_pairs={{0,16},{16,0},{1,17},{17,1},{2,18},{18,2},{3,19},{19,3},{4,20},{20... | collective-permute-start | bytes 3096584 | tf_op jit(solution)/shard_map/ppermute | solution.py:38
  54.5 19.8 %collective-permute-start.8 = (bf16[128,512]{1,0:T(8,128)(2,1)S(1)}, bf16[128,512]{1,0:T(8,128)(2,1)S(1)}, u32[]{:S(2)}, u32[]{:S(2)}) collective-permute-start(bf16[128,512]{1,0:T(8,128)(2,1)S(1)} %copy-done.12), channel_id=1, source_target_pairs={{0,2},{1,3},{2,0},{3,1},{4,6},{5,7},{6,4},{7,5},{8,10},{9,11},{10,... | collective-permute-start | bytes 393224 | tf_op jit(solution)/shard_map/ppermute | solution.py:38
  56.0 18.3 %collective-permute-start.9 = (bf16[128,512]{1,0:T(8,128)(2,1)S(1)}, bf16[128,512]{1,0:T(8,128)(2,1)S(1)}, u32[]{:S(2)}, u32[]{:S(2)}) collective-permute-start(bf16[128,512]{1,0:T(8,128)(2,1)S(1)} %copy-done.12), channel_id=1, source_target_pairs={{0,1},{1,0},{2,3},{3,2},{4,5},{5,4},{6,7},{7,6},{8,9},{9,8},{10,11... | collective-permute-start | bytes 393224 | tf_op jit(solution)/shard_map/ppermute | solution.py:38
  74.3 48.3 %collective-permute-start.12 = (bf16[128,2048]{1,0:T(8,128)(2,1)S(1)}, bf16[128,2048]{1,0:T(8,128)(2,1)}, u32[]{:S(2)}, u32[]{:S(2)}) collective-permute-start(bf16[128,2048]{1,0:T(8,128)(2,1)S(1)} %copy-done.10), channel_id=1, source_target_pairs={{0,1},{1,0},{2,3},{3,2},{4,5},{5,4},{6,7},{7,6},{8,9},{9,8},{10,11... | collective-permute-start | bytes 1572872 | tf_op jit(solution)/shard_map/ppermute | solution.py:38
  74.3 48.3 %collective-permute-start.15 = (bf16[512,512]{1,0:T(8,128)(2,1)}, bf16[512,512]{1,0:T(8,128)(2,1)}, u32[]{:S(2)}, u32[]{:S(2)}) collective-permute-start(bf16[512,512]{1,0:T(8,128)(2,1)} %rest_8_), channel_id=1, source_target_pairs={{0,1},{1,0},{2,3},{3,2},{4,5},{5,4},{6,7},{7,6},{8,9},{9,8},{10,11... | collective-permute-start | bytes 1572872 | tf_op jit(solution)/shard_map/ppermute | solution.py:38
  74.8 47.8 %collective-permute-start.13 = (bf16[128,2048]{1,0:T(8,128)(2,1)}, bf16[128,2048]{1,0:T(8,128)(2,1)}, u32[]{:S(2)}, u32[]{:S(2)}) collective-permute-start(bf16[128,2048]{1,0:T(8,128)(2,1)} %collective-permute-done.11.rest_5_), channel_id=1, source_target_pairs={{0,1},{1,0},{2,3},{3,2},{4,5},{5,4},{6,7},{7,6},{8,9},{9,8},{10,11... | collective-permute-start | bytes 1572872 | tf_op jit(solution)/shard_map/ppermute | solution.py:38
  74.9 47.8 %collective-permute-start.16 = (bf16[512,512]{1,0:T(8,128)(2,1)}, bf16[512,512]{1,0:T(8,128)(2,1)}, u32[]{:S(2)}, u32[]{:S(2)}) collective-permute-start(bf16[512,512]{1,0:T(8,128)(2,1)} %collective-permute-done.14.rest_9_), channel_id=1, source_target_pairs={{0,1},{1,0},{2,3},{3,2},{4,5},{5,4},{6,7},{7,6},{8,9},{9,8},{10,11... | collective-permute-start | bytes 1572872 | tf_op jit(solution)/shard_map/ppermute | solution.py:38
  82.1 40.5 %collective-permute-start.10 = (bf16[128,512]{1,0:T(8,128)(2,1)S(1)}, bf16[128,512]{1,0:T(8,128)(2,1)S(1)}, u32[]{:S(2)}, u32[]{:S(2)}) collective-permute-start(bf16[128,512]{1,0:T(8,128)(2,1)S(1)} %copy-done.14), channel_id=1, source_target_pairs={{0,1},{1,0},{2,3},{3,2},{4,5},{5,4},{6,7},{7,6},{8,9},{9,8},{10,11... | collective-permute-start | bytes 393224 | tf_op jit(solution)/shard_map/ppermute | solution.py:38
  274.3 64.1 %collective-permute-start.39 = (bf16[2,512,512]{2,1,0:T(8,128)(2,1)S(1)}, bf16[2,512,512]{2,1,0:T(8,128)(2,1)}, u32[]{:S(2)}, u32[]{:S(2)}) collective-permute-start(bf16[2,512,512]{2,1,0:T(8,128)(2,1)S(1)} %dynamic-slice_bitcast_fusion), channel_id=1, source_target_pairs={{0,1},{1,0},{2,3},{3,2},{4,5},{5,4},{6,7},{7,6},{8,9},{9,8},{10,11... | collective-permute-start | bytes 3145736 | tf_op jit(solution)/shard_map/ppermute | solution.py:38
  279.0 12.7 %collective-permute-start.24 = (bf16[2,128,1536]{2,1,0:T(8,128)(2,1)}, bf16[2,128,1536]{2,1,0:T(8,128)(2,1)}, u32[]{:S(2)}, u32[]{:S(2)}) collective-permute-start(bf16[2,128,1536]{2,1,0:T(8,128)(2,1)} %dynamic-slice_bitcast_fusion.2), channel_id=1, source_target_pairs={{0,1},{1,0},{2,3},{3,2},{4,5},{5,4},{6,7},{7,6},{8,9},{9,8},{10,11... | collective-permute-start | bytes 2359304 | tf_op jit(solution)/shard_map/ppermute | solution.py:38
  284.6 57.0 %collective-permute-start.34 = (bf16[2,128,2048]{2,1,0:T(8,128)(2,1)}, bf16[2,128,2048]{2,1,0:T(8,128)(2,1)}, u32[]{:S(2)}, u32[]{:S(2)}) collective-permute-start(bf16[2,128,2048]{2,1,0:T(8,128)(2,1)} %dynamic-slice_bitcast_fusion.1), channel_id=1, source_target_pairs={{0,1},{1,0},{2,3},{3,2},{4,5},{5,4},{6,7},{7,6},{8,9},{9,8},{10,11... | collective-permute-start | bytes 3145736 | tf_op jit(solution)/shard_map/ppermute | solution.py:38
  287.6 26.0 %collective-permute-start.18 = (bf16[24,3,14,512]{3,0,2,1:T(8,128)(2,1)}, bf16[24,3,14,512]{3,0,2,1:T(8,128)(2,1)}, u32[]{:S(2)}, u32[]{:S(2)}) collective-permute-start(bf16[24,3,14,512]{3,0,2,1:T(8,128)(2,1)} %copy.81), channel_id=1, source_target_pairs={{0,16},{16,0},{1,17},{17,1},{2,18},{18,2},{3,19},{19,3},{4,20},{20... | collective-permute-start | bytes 3096584 | tf_op jit(solution)/shard_map/ppermute | solution.py:38
  291.1 44.1 %collective-permute-start.17 = (bf16[24,3,14,512]{3,0,2,1:T(8,128)(2,1)}, bf16[24,3,14,512]{3,0,2,1:T(8,128)(2,1)S(1)}, u32[]{:S(2)}, u32[]{:S(2)}) collective-permute-start(bf16[24,3,14,512]{3,0,2,1:T(8,128)(2,1)} %copy.78), channel_id=1, source_target_pairs={{0,16},{16,0},{1,17},{17,1},{2,18},{18,2},{3,19},{19,3},{4,20},{20... | collective-permute-start | bytes 3096584 | tf_op jit(solution)/shard_map/ppermute | solution.py:38
  300.7 43.0 %collective-permute-start.25 = (bf16[1,128,1536]{2,1,0:T(8,128)(2,1)S(1)}, bf16[1,128,1536]{2,1,0:T(8,128)(2,1)S(1)}, u32[]{:S(2)}, u32[]{:S(2)}) collective-permute-start(bf16[1,128,1536]{2,1,0:T(8,128)(2,1)S(1)} %constant_dynamic-slice_fusion.10), channel_id=1, source_target_pairs={{0,2},{1,3},{2,0},{3,1},{4,6},{5,7},{6,4},{7,5},{8,10},{9,11},{10,... | collective-permute-start | bytes 1179656 | tf_op jit(solution)/shard_map/ppermute | solution.py:38
  340.0 14.9 %collective-permute-start.40 = (bf16[1,512,512]{2,1,0:T(8,128)(2,1)S(1)}, bf16[1,512,512]{2,1,0:T(8,128)(2,1)S(1)}, u32[]{:S(2)}, u32[]{:S(2)}) collective-permute-start(bf16[1,512,512]{2,1,0:T(8,128)(2,1)S(1)} %constant_dynamic-slice_fusion.7), channel_id=1, source_target_pairs={{0,2},{1,3},{2,0},{3,1},{4,6},{5,7},{6,4},{7,5},{8,10},{9,11},{10,... | collective-permute-start | bytes 1572872 | tf_op jit(solution)/shard_map/ppermute | solution.py:38
  343.2 21.5 %collective-permute-start.35 = (bf16[1,128,2048]{2,1,0:T(8,128)(2,1)S(1)}, bf16[1,128,2048]{2,1,0:T(8,128)(2,1)S(1)}, u32[]{:S(2)}, u32[]{:S(2)}) collective-permute-start(bf16[1,128,2048]{2,1,0:T(8,128)(2,1)S(1)} %constant_dynamic-slice_fusion.8), channel_id=1, source_target_pairs={{0,2},{1,3},{2,0},{3,1},{4,6},{5,7},{6,4},{7,5},{8,10},{9,11},{10,... | collective-permute-start | bytes 1572872 | tf_op jit(solution)/shard_map/ppermute | solution.py:38
  343.9 22.5 %collective-permute-start.26 = (bf16[128,1536]{1,0:T(8,128)(2,1)S(1)}, bf16[128,1536]{1,0:T(8,128)(2,1)S(1)}, u32[]{:S(2)}, u32[]{:S(2)}) collective-permute-start(bf16[128,1536]{1,0:T(8,128)(2,1)S(1)} %fusion.29), channel_id=1, source_target_pairs={{0,16},{16,0},{1,17},{17,1},{2,18},{18,2},{3,19},{19,3},{4,20},{20... | collective-permute-start | bytes 1179656 | tf_op jit(solution)/shard_map/ppermute | solution.py:38
  355.0 12.1 %collective-permute-start.41 = (bf16[512,512]{1,0:T(8,128)(2,1)S(1)}, bf16[512,512]{1,0:T(8,128)(2,1)S(1)}, u32[]{:S(2)}, u32[]{:S(2)}) collective-permute-start(bf16[512,512]{1,0:T(8,128)(2,1)S(1)} %fusion.26), channel_id=1, source_target_pairs={{0,16},{16,0},{1,17},{17,1},{2,18},{18,2},{3,19},{19,3},{4,20},{20... | collective-permute-start | bytes 1572872 | tf_op jit(solution)/shard_map/ppermute | solution.py:38
  364.9 12.7 %collective-permute-start.36 = (bf16[128,2048]{1,0:T(8,128)(2,1)S(1)}, bf16[128,2048]{1,0:T(8,128)(2,1)S(1)}, u32[]{:S(2)}, u32[]{:S(2)}) collective-permute-start(bf16[128,2048]{1,0:T(8,128)(2,1)S(1)} %fusion.24), channel_id=1, source_target_pairs={{0,16},{16,0},{1,17},{17,1},{2,18},{18,2},{3,19},{19,3},{4,20},{20... | collective-permute-start | bytes 1572872 | tf_op jit(solution)/shard_map/ppermute | solution.py:38
  366.5 12.1 %collective-permute-start.27 = (bf16[128,1536]{1,0:T(8,128)(2,1)S(1)}, bf16[128,1536]{1,0:T(8,128)(2,1)S(1)}, u32[]{:S(2)}, u32[]{:S(2)}) collective-permute-start(bf16[128,1536]{1,0:T(8,128)(2,1)S(1)} %add_convert_fusion.10), channel_id=1, source_target_pairs={{0,4},{4,0},{8,12},{12,8},{1,5},{5,1},{9,13},{13,9},{2,6},{6,2},{1... | collective-permute-start | bytes 1179656 | tf_op jit(solution)/shard_map/ppermute | solution.py:38
  367.2 32.2 %collective-permute-start.42 = (bf16[512,512]{1,0:T(8,128)(2,1)S(1)}, bf16[512,512]{1,0:T(8,128)(2,1)S(1)}, u32[]{:S(2)}, u32[]{:S(2)}) collective-permute-start(bf16[512,512]{1,0:T(8,128)(2,1)S(1)} %add_convert_fusion.2), channel_id=1, source_target_pairs={{0,4},{4,0},{8,12},{12,8},{1,5},{5,1},{9,13},{13,9},{2,6},{6,2},{1... | collective-permute-start | bytes 1572872 | tf_op jit(solution)/shard_map/ppermute | solution.py:38
  377.7 31.8 %collective-permute-start.37 = (bf16[128,2048]{1,0:T(8,128)(2,1)S(1)}, bf16[128,2048]{1,0:T(8,128)(2,1)S(1)}, u32[]{:S(2)}, u32[]{:S(2)}) collective-permute-start(bf16[128,2048]{1,0:T(8,128)(2,1)S(1)} %add_convert_fusion.6), channel_id=1, source_target_pairs={{0,4},{4,0},{8,12},{12,8},{1,5},{5,1},{9,13},{13,9},{2,6},{6,2},{1... | collective-permute-start | bytes 1572872 | tf_op jit(solution)/shard_map/ppermute | solution.py:38
  378.7 31.0 %collective-permute-start.28 = (bf16[128,1536]{1,0:T(8,128)(2,1)S(1)}, bf16[128,1536]{1,0:T(8,128)(2,1)S(1)}, u32[]{:S(2)}, u32[]{:S(2)}) collective-permute-start(bf16[128,1536]{1,0:T(8,128)(2,1)S(1)} %add_convert_fusion.9), channel_id=1, source_target_pairs={{0,8},{4,12},{8,0},{12,4},{1,9},{5,13},{9,1},{13,5},{2,10},{6,14},... | collective-permute-start | bytes 1179656 | tf_op jit(solution)/shard_map/ppermute | solution.py:38
  399.5 42.1 %collective-permute-start.43 = (bf16[512,512]{1,0:T(8,128)(2,1)S(1)}, bf16[512,512]{1,0:T(8,128)(2,1)S(1)}, u32[]{:S(2)}, u32[]{:S(2)}) collective-permute-start(bf16[512,512]{1,0:T(8,128)(2,1)S(1)} %add_convert_fusion.1), channel_id=1, source_target_pairs={{0,8},{4,12},{8,0},{12,4},{1,9},{5,13},{9,1},{13,5},{2,10},{6,14},... | collective-permute-start | bytes 1572872 | tf_op jit(solution)/shard_map/ppermute | solution.py:38
  409.6 40.8 %collective-permute-start.38 = (bf16[128,2048]{1,0:T(8,128)(2,1)S(1)}, bf16[128,2048]{1,0:T(8,128)(2,1)S(1)}, u32[]{:S(2)}, u32[]{:S(2)}) collective-permute-start(bf16[128,2048]{1,0:T(8,128)(2,1)S(1)} %add_convert_fusion.5), channel_id=1, source_target_pairs={{0,8},{4,12},{8,0},{12,4},{1,9},{5,13},{9,1},{13,5},{2,10},{6,14},... | collective-permute-start | bytes 1572872 | tf_op jit(solution)/shard_map/ppermute | solution.py:38
  (35 other events, 665.3 us)
